TPU v7x, 32 devices: a whole 2x2x4 slice. The times are simulated.
32 devices in a mesh: scan: 8 (over z, x), col: 4 (over y, core).
Axes of the slice: x: 2, y: 2, z: 4, core: 2. Of those that a mesh axis runs over, the one named last changes fastest.
Arguments:
- object_field: float32 [2, 2048, 1024], P(None, 'scan', 'col'), may hold values from -6 to 6
- amplitudes: bfloat16 [64, 256, 256], P(('scan', 'col')), may hold values from 0.099609375 to 3
- positions: int32 [64, 2], P(('scan', 'col')), may hold values from 0 to 1792, as said below
- frame_count: int32 [32], P(('scan', 'col')), may hold values from 1 to 2, as said below
- coefficients: float32 [64, 4], P(('scan', 'col')), may hold values from -6 to 6
- probe_modes: float32 [4, 2, 256, 256], replicated, may hold values from -6 to 6
Outputs:
- refined_object: float32 [2, 2048, 1024], P(None, 'scan', 'col')
- refined_modes: float32 [4, 2, 256, 256], replicated
- refined_coefficients: float32 [64, 4], P(('scan', 'col'))
Inputs may be any that keep to these rules, and one draw needn't show every extreme that they name: `positions`: frame g belongs to the device of index g // 2 along scan+col (scan slowest). Its top-left pixel lies in that device's block of 256 x 256 pixels, and its 256 x 256 patch lies inside the object. Entry d counts the live frames of the device of index d along scan+col: its first frame_count[d] slots are live, the rest are ignored. Some device has 2.
All inputs are finite; a program needn't handle non-finite values.
Results may differ from a plain program's by a relative error of at most 0.0058.
Values sent between devices are 32-bit elements; how exact they have to be, the bound alone decides.
A program may use at most 128 MiB of HBM per device.

v0:
```python
import math

import jax
import jax.numpy as jnp
from jax import lax
from jax.sharding import PartitionSpec as P

ITERS = 2


highest = lax.Precision.HIGHEST


def from_behind(shard, axis, by):
    size = lax.axis_size(axis)
    pairs = [(i, i + by) for i in range(size) if 0 <= i + by < size]
    return lax.ppermute(shard, axis, pairs)


def make_tables(length):
    indices = jnp.arange(length, dtype=jnp.int32)
    phases = indices[:, None] * indices[None, :] % length
    angles = phases.astype(jnp.float32) * (2.0 * math.pi / length)
    factor = 1.0 / math.sqrt(length)
    cosine = jnp.cos(angles) * factor
    sine_table = jnp.sin(angles) * factor
    rows_table = jnp.concatenate(
        [jnp.concatenate([cosine, sine_table], 1), jnp.concatenate([-sine_table, cosine], 1)], 0
    )
    cols_table = jnp.concatenate(
        [jnp.concatenate([cosine, -sine_table], 1), jnp.concatenate([sine_table, cosine], 1)], 0
    )
    return (rows_table.astype(jnp.bfloat16), cols_table.astype(jnp.bfloat16))


def apply_transform(real_part, imag_part, first_table, second_table):
    length = real_part.shape[0]
    stacked = jnp.concatenate([real_part, imag_part], 0)
    halfway = jnp.dot(first_table, stacked, preferred_element_type=jnp.float32).astype(jnp.bfloat16)
    beside = jnp.concatenate([halfway[:length], halfway[length:]], 1)
    result = jnp.dot(beside, second_table, preferred_element_type=jnp.float32)
    return (result[:, :length], result[:, length:])


def frame_update(object_patch, probe_field, amplitude, rows_table, cols_table):
    probe_real = probe_field[0]
    probe_imag = probe_field[1]
    object_real = object_patch[0]
    object_imag = object_patch[1]
    exit_real = probe_real * object_real - probe_imag * object_imag
    exit_imag = probe_real * object_imag + probe_imag * object_real
    far_real, far_imag = apply_transform(
        exit_real.astype(jnp.bfloat16), exit_imag.astype(jnp.bfloat16), rows_table, cols_table
    )
    magnitude = jnp.sqrt(far_real * far_real + far_imag * far_imag)
    factor = amplitude.astype(jnp.float32) / jnp.maximum(magnitude, 0.5)
    new_real, new_imag = apply_transform(
        (far_real * factor).astype(jnp.bfloat16),
        (far_imag * factor).astype(jnp.bfloat16),
        cols_table,
        rows_table,
    )
    diff_real = new_real - exit_real
    diff_imag = new_imag - exit_imag
    update = jnp.stack(
        [
            probe_real * diff_real + probe_imag * diff_imag,
            probe_real * diff_imag - probe_imag * diff_real,
            probe_real * probe_real + probe_imag * probe_imag,
        ]
    )
    probe_step = jnp.stack(
        [
            object_real * diff_real + object_imag * diff_imag,
            object_real * diff_imag - object_imag * diff_real,
        ]
    )
    return (update, probe_step)


def gram_parts(flat_modes):
    real_plane = flat_modes[:, 0]
    imag_plane = flat_modes[:, 1]
    gram_real = jnp.dot(
        real_plane, real_plane.T, precision=highest, preferred_element_type=jnp.float32
    ) + jnp.dot(imag_plane, imag_plane.T, precision=highest, preferred_element_type=jnp.float32)
    gram_imag = jnp.dot(
        real_plane, imag_plane.T, precision=highest, preferred_element_type=jnp.float32
    ) - jnp.dot(imag_plane, real_plane.T, precision=highest, preferred_element_type=jnp.float32)
    return (gram_real, gram_imag)


def orthonormal(flat_modes, gram_real, gram_imag):
    mode_count = flat_modes.shape[0]
    upper_real = [[None] * mode_count for other in range(mode_count)]
    upper_imag = [[None] * mode_count for other in range(mode_count)]
    for right_index in range(mode_count):
        for left_index in range(right_index):
            sum_real = gram_real[left_index, right_index]
            sum_imag = gram_imag[left_index, right_index]
            for inner_index in range(left_index):
                first_real = upper_real[inner_index][left_index]
                first_imag = upper_imag[inner_index][left_index]
                second_real = upper_real[inner_index][right_index]
                second_imag = upper_imag[inner_index][right_index]
                sum_real = sum_real - (first_real * second_real + first_imag * second_imag)
                sum_imag = sum_imag - (first_real * second_imag - first_imag * second_real)
            upper_real[left_index][right_index] = sum_real / upper_real[left_index][left_index]
            upper_imag[left_index][right_index] = sum_imag / upper_real[left_index][left_index]
        diagonal = gram_real[right_index, right_index]
        for inner_index in range(right_index):
            entry_real = upper_real[inner_index][right_index]
            entry_imag = upper_imag[inner_index][right_index]
            diagonal = diagonal - (entry_real * entry_real + entry_imag * entry_imag)
        upper_real[right_index][right_index] = jnp.sqrt(diagonal)
    columns = []
    for right_index in range(mode_count):
        vector_real = flat_modes[right_index, 0]
        vector_imag = flat_modes[right_index, 1]
        for left_index in range(right_index):
            basis_real, basis_imag = columns[left_index]
            entry_real = upper_real[left_index][right_index]
            entry_imag = upper_imag[left_index][right_index]
            vector_real = vector_real - (entry_real * basis_real - entry_imag * basis_imag)
            vector_imag = vector_imag - (entry_real * basis_imag + entry_imag * basis_real)
        pivot = upper_real[right_index][right_index]
        columns.append((vector_real / pivot, vector_imag / pivot))
    return jnp.stack([jnp.stack([pair[0], pair[1]]) for pair in columns])


def widen(object_field, col_index, col_count):
    lower_rim = from_behind(object_field, "scan", -1)
    beyond = from_behind(object_field, "col", -1)
    corner = from_behind(object_field, ("scan", "col"), -(col_count + 1))
    corner = jnp.where(col_index < col_count - 1, corner, jnp.zeros_like(corner))
    upper_band = jnp.concatenate([object_field, beyond], 2)
    bottom = jnp.concatenate([lower_rim, corner], 2)
    extended = jnp.concatenate([upper_band, bottom], 1)
    return extended


def settle(totals, block_height, block_width, length, col_index, col_count):
    arrived = from_behind(totals[:, :block_height, block_width:], "col", 1)
    lowered = from_behind(totals[:, block_height:, :block_width], "scan", 1)
    corner = from_behind(totals[:, block_height:, block_width:], ("scan", "col"), col_count + 1)
    corner = jnp.where(col_index > 0, corner, jnp.zeros_like(corner))
    settled = totals[:, :block_height, :block_width]
    settled = settled.at[:, :, :length].add(arrived)
    settled = settled.at[:, :length, :].add(lowered)
    settled = settled.at[:, :length, :length].add(corner)
    return settled


def on_device(object_field, amplitudes, positions, frame_count, coefficients, probe_modes):
    frames = amplitudes.shape[0]
    length = amplitudes.shape[1]
    mode_count = probe_modes.shape[0]
    block_height = object_field.shape[1]
    block_width = object_field.shape[2]
    scan_count = lax.axis_size("scan")
    col_count = lax.axis_size("col")
    col_index = lax.axis_index("col")
    block_corner = jnp.stack([lax.axis_index("scan") * block_height, col_index * block_width])
    local_offsets = positions - block_corner[None, :]
    pixels = length * length
    root_total = math.sqrt(frames * scan_count * col_count)
    rows_table, cols_table = make_tables(length)
    live_count = frame_count[0]
    slot_index = jnp.arange(frames, dtype=jnp.int32)
    live_mask = slot_index < live_count
    anchor = jnp.zeros((), jnp.int32)
    for iteration in range(ITERS):
        extended = widen(object_field, col_index, col_count)
        current_modes = probe_modes
        current_weights = coefficients

        def visit(frame_slot, state):
            totals, mode_terms, stashed = state
            offset = local_offsets[frame_slot]
            weights = current_weights[frame_slot]
            object_patch = lax.dynamic_slice(
                extended, (anchor, offset[0], offset[1]), (2, length, length)
            )
            probe_field = jnp.tensordot(weights, current_modes, axes=1, precision=highest)
            update, probe_step = frame_update(
                object_patch, probe_field, amplitudes[frame_slot], rows_table, cols_table
            )
            window = lax.dynamic_slice(totals, (anchor, offset[0], offset[1]), (3, length, length))
            totals = lax.dynamic_update_slice(
                totals, window + update, (anchor, offset[0], offset[1])
            )
            mode_terms = mode_terms + weights[:, None, None, None] * probe_step[None]
            stashed = lax.dynamic_update_slice(
                stashed, probe_step[None], (frame_slot, anchor, anchor, anchor)
            )
            return (totals, mode_terms, stashed)

        initial = (
            jnp.zeros((3, block_height + length, block_width + length), jnp.float32),
            jnp.zeros((mode_count, 2, length, length), jnp.float32),
            jnp.zeros((frames, 2, length, length), jnp.float32),
        )
        totals, mode_terms, stashed = lax.fori_loop(0, live_count, visit, initial)
        settled = settle(totals, block_height, block_width, length, col_index, col_count)
        object_field = object_field + settled[:2] / (settled[2] + 1.0)
        summed = lax.psum(mode_terms, ("scan", "col"))
        raised = (probe_modes + summed / root_total).reshape(mode_count, 2, pixels)
        gram_real, gram_imag = gram_parts(raised)
        orthogonal = orthonormal(raised, gram_real / pixels, gram_imag / pixels)
        ortho_flat = orthogonal.reshape(mode_count, 2 * pixels)
        mixing = (
            jnp.dot(
                probe_modes.reshape(mode_count, 2 * pixels),
                ortho_flat.T,
                precision=highest,
                preferred_element_type=jnp.float32,
            )
            / pixels
        )
        projected = (
            jnp.dot(
                stashed.reshape(frames, 2 * pixels),
                ortho_flat.T,
                precision=highest,
                preferred_element_type=jnp.float32,
            )
            / pixels
        )
        refit = (
            jnp.dot(coefficients, mixing, precision=highest, preferred_element_type=jnp.float32)
            + 0.5 * projected
        )
        coefficients = jnp.where(live_mask[:, None], refit, coefficients)
        probe_modes = orthogonal.reshape(mode_count, 2, length, length)
    return (object_field, probe_modes, coefficients)


def solution(mesh):
    placed = (
        P(None, "scan", "col"),
        P(("scan", "col"), None, None),
        P(("scan", "col"), None),
        P(("scan", "col")),
        P(("scan", "col"), None),
        P(),
    )
    return jax.shard_map(
        on_device,
        mesh=mesh,
        in_specs=placed,
        out_specs=(P(None, "scan", "col"), P(), P(("scan", "col"), None)),
        check_vma=False,
    )
```

profile of v0, /device:TPU:0, one launch (start us, length us, event | category | flops | bytes accessed | tf_op | source)
XLA Modules:
  0.0 628.5 jit_solution(5073344598730593625)
XLA Ops:
  15.0 15.0 %collective-permute-done.2 = f32[2,256,256]{2,1,0:T(8,128)S(1)} collective-permute-done((f32[2,256,256]{2,1,0:T(8,128)}, f32[2,256,256]{2,1,0:T(8,128)S(1)}, u32[]{:S(2)}, u32[]{:S(2)}) %collective-permute-start.2) | collective-permute-done | bytes 524320 | tf_op jit(solution)/shard_map/ppermute | solution.py:17
  36.4 30.8 %while.40 = (s32[]{:T(128)}, f32[3,512,512]{2,1,0:T(8,128)}, f32[4,2,256,256]{3,2,1,0:T(8,128)}, f32[2,2,256,256]{3,2,1,0:T(8,128)}, s32[]{:T(128)}, /*index=5*/...) while((s32[]{:T(128)}, f32[3,512,512]{2,1,0:T(8,128)}, ...), condition=%wide.region_1.2_spmd, body=%wide.region_0.1_spmd.sunk | while | flops 549715968 | bytes 36832196 | solution.py:203
  41.7 4.3 fusion.272
  57.1 9.4 %dynamic_update_slice.19 = f32[3,512,512]{2,1,0:T(8,128)} dynamic-update-slice(f32[3,512,512]{2,1,0:T(8,128)} %get-tuple-element.683, f32[3,256,256]{2,1,0:T(8,128)S(1)} %maximum_add_fusion.4, s32[]{:T(128)} %constant.254.clone.1..sunk, s32[]{:T(128)S(6)} %select_n.121, s32[]{:T(128)S(6)} %select_n.122) | dynamic-update-slice | bytes 1572868 | tf_op jit(solution)/shard_map/while/body/dynamic_update_slice | solution.py:189
  70.2 9.5 %collective-permute-start.3 = (f32[3,256,256]{2,1,0:T(8,128)}, f32[3,256,256]{2,1,0:T(8,128)}, u32[]{:S(2)}, u32[]{:S(2)}) collective-permute-start(f32[3,256,256]{2,1,0:T(8,128)} %get-tuple-element.382), channel_id=1, source_target_pairs={{0,1},{1,2},{2,3},{4,5},{5,6},{6,7},{8,9},{9,10},{10,11},{12,13},{... | collective-permute-start | bytes 2359304 | tf_op jit(solution)/shard_map/ppermute | solution.py:17
  79.7 33.0 %collective-permute-start.5 = (f32[3,256,256]{2,1,0:T(8,128)}, f32[3,256,256]{2,1,0:T(8,128)}, u32[]{:S(2)}, u32[]{:S(2)}) collective-permute-start(f32[3,256,256]{2,1,0:T(8,128)} %get-tuple-element.383), channel_id=1, source_target_pairs={{0,5},{1,6},{2,7},{3,8},{4,9},{5,10},{6,11},{7,12},{8,13},{9,14},{... | collective-permute-start | bytes 2359304 | tf_op jit(solution)/shard_map/ppermute | solution.py:17
  112.7 3.4 collective-permute-start.4
  122.6 10.4 %collective-permute-done.5 = f32[3,256,256]{2,1,0:T(8,128)} collective-permute-done((f32[3,256,256]{2,1,0:T(8,128)}, f32[3,256,256]{2,1,0:T(8,128)}, u32[]{:S(2)}, u32[]{:S(2)}) %collective-permute-start.5) | collective-permute-done | bytes 786464 | tf_op jit(solution)/shard_map/ppermute | solution.py:17
  133.1 9.5 %collective-permute-done.4 = f32[3,256,256]{2,1,0:T(8,128)} collective-permute-done((f32[3,256,256]{2,1,0:T(8,128)S(1)}, f32[3,256,256]{2,1,0:T(8,128)}, u32[]{:S(2)}, u32[]{:S(2)}) %collective-permute-start.4) | collective-permute-done | bytes 786464 | tf_op jit(solution)/shard_map/ppermute | solution.py:17
  148.4 101.9 %all-reduce.3.cloned.1.call-done = f32[4,2,256,256]{3,2,1,0:T(8,128)} async-done(((f32[4,2,256,256]{3,2,1,0:T(8,128)}), f32[4,2,256,256]{3,2,1,0:T(8,128)}) %all-reduce.3.cloned.1.call-update) | async-done | bytes 2097168 | tf_op jit(solution)/shard_map/psum | solution.py:206
  257.0 4.7 slice_reduce_fusion.7
  263.3 4.7 fusion.105
  268.0 5.4 fusion.100
  273.4 5.0 fusion.78
  278.4 4.7 fusion.79
  303.8 3.6 fusion.151
  316.0 10.0 %convolution_multiply_fusion = f32[4,4]{1,0:T(4,128)S(1)} fusion(f32[4,131072]{1,0:T(4,128)S(1)} %bitcast.607, f32[1,131072]{1,0:T(1,128)S(1)} %bitcast.614, f32[1,131072]{1,0:T(1,128)S(1)} %bitcast.618, f32[1,131072]{1,0:T(1,128)S(1)} %bitcast.620, f32[1,131072]{1,0:T(1,128)S(1)} %bitcast.616), kind=kOutput, calls=%fused_computation.139 | convolution fusion | flops 26738704 | bytes 4194368 | tf_op jit(solution)/shard_map/dot_general | solution.py:212
  326.0 9.5 %convolution_multiply_fusion.1 = f32[2,4]{1,0:T(2,128)S(1)} fusion(f32[2,131072]{1,0:T(2,128)S(1)} %bitcast.609, f32[1,131072]{1,0:T(1,128)S(1)} %bitcast.615, f32[1,131072]{1,0:T(1,128)S(1)} %bitcast.619, f32[1,131072]{1,0:T(1,128)S(1)} %bitcast.621, f32[1,131072]{1,0:T(1,128)S(1)} %bitcast.617), kind=kOutput, calls=%fused_computation.145 | convolution fusion | flops 14155784 | bytes 3145760 | tf_op jit(solution)/shard_map/dot_general | solution.py:221
  346.2 30.4 %while.41 = (s32[]{:T(128)}, f32[3,512,512]{2,1,0:T(8,128)}, f32[4,2,256,256]{3,2,1,0:T(8,128)S(1)}, f32[2,2,256,256]{3,2,1,0:T(8,128)}, s32[]{:T(128)}, /*index...) while((s32[]{:T(128)}, f32[3,512,512]{2,1,0:T(8,128)}, ...), condition=%wide.region_4.5_spmd, body=%wide.region_3.4_spmd.sunk | while | flops 549715968 | bytes 36832196 | solution.py:203
  351.5 6.7 %fusion.293 = f32[1,2,256,256]{3,0,2,1:T(1,128)S(1)} fusion(f32[4,2,256,256]{3,2,1,0:T(8,128)} %get-tuple-element.757, f32[2,4]{1,0:T(2,128)S(1)} %get-tuple-element.756, s32[]{:T(128)S(6)} %select_n.123), kind=kOutput, calls=%fused_computation.57.clone.1 | convolution fusion | flops 6291456 | bytes 2621956 | tf_op jit(solution)/shard_map/while/body/dot_general | solution.py:184
  366.6 9.4 %dynamic_update_slice.21 = f32[3,512,512]{2,1,0:T(8,128)} dynamic-update-slice(f32[3,512,512]{2,1,0:T(8,128)} %get-tuple-element.734, f32[3,256,256]{2,1,0:T(8,128)S(1)} %maximum_add_fusion.5, s32[]{:T(128)} %constant.254.clone.1..sunk.1, s32[]{:T(128)S(6)} %select_n.124, s32[]{:T(128)S(6)} %select_n.125) | dynamic-update-slice | bytes 1572868 | tf_op jit(solution)/shard_map/while/body/dynamic_update_slice | solution.py:189
  381.3 31.1 %collective-permute-start.11 = (f32[3,256,256]{2,1,0:T(8,128)S(1)}, f32[3,256,256]{2,1,0:T(8,128)S(1)}, u32[]{:S(2)}, u32[]{:S(2)}) collective-permute-start(f32[3,256,256]{2,1,0:T(8,128)S(1)} %get-tuple-element.380), channel_id=1, source_target_pairs={{0,5},{1,6},{2,7},{3,8},{4,9},{5,10},{6,11},{7,12},{8,13},{9,14},{... | collective-permute-start | bytes 2359304 | tf_op jit(solution)/shard_map/ppermute | solution.py:17
  419.4 11.6 %collective-permute-done.11 = f32[3,256,256]{2,1,0:T(8,128)S(1)} collective-permute-done((f32[3,256,256]{2,1,0:T(8,128)S(1)}, f32[3,256,256]{2,1,0:T(8,128)S(1)}, u32[]{:S(2)}, u32[]{:S(2)}) %collective-permute-start.11) | collective-permute-done | bytes 786464 | tf_op jit(solution)/shard_map/ppermute | solution.py:17
  431.0 10.8 %collective-permute-done.10 = f32[3,256,256]{2,1,0:T(8,128)S(1)} collective-permute-done((f32[3,256,256]{2,1,0:T(8,128)S(1)}, f32[3,256,256]{2,1,0:T(8,128)S(1)}, u32[]{:S(2)}, u32[]{:S(2)}) %collective-permute-start.10) | collective-permute-done | bytes 786464 | tf_op jit(solution)/shard_map/ppermute | solution.py:17
  444.2 95.4 %all-reduce.5.cloned.1.call-done = f32[4,2,256,256]{3,2,1,0:T(8,128)} async-done(((f32[4,2,256,256]{3,2,1,0:T(8,128)}), f32[4,2,256,256]{3,2,1,0:T(8,128)}) %all-reduce.5.cloned.1.call-update) | async-done | bytes 2097168 | tf_op jit(solution)/shard_map/psum | solution.py:206
  546.2 4.0 slice_reduce_fusion.1
  551.8 4.7 fusion.97
  556.5 5.4 fusion.92
  561.9 5.0 fusion.76
  566.9 4.7 fusion.77
  598.4 11.0 %fusion.80 = f32[4,4]{1,0:T(4,128)S(1)} fusion(f32[4,2,65536]{2,1,0:T(2,128)S(1)} %pad_maximum_fusion.4, f32[4,2,65536]{2,1,0:T(2,128)S(1)} %copy-done.4), kind=kOutput, calls=%fused_computation.144 | convolution fusion | flops 25165840 | bytes 4194368 | tf_op jit(solution)/shard_map/dot_general | solution.py:212
  609.4 9.7 %fusion.88 = f32[2,4]{1,0:T(2,128)S(1)} fusion(f32[2,131072]{1,0:T(2,128)S(1)} %bitcast.608, f32[1,131072]{1,0:T(1,128)S(1)} %bitcast.610, f32[1,131072]{1,0:T(1,128)S(1)} %bitcast.612, f32[1,131072]{1,0:T(1,128)S(1)} %bitcast.613, f32[1,131072]{1,0:T(1,128)S(1)} %bitcast.611), kind=kOutput, calls=%fused_computation.151 | convolution fusion | flops 14155784 | bytes 3145760 | tf_op jit(solution)/shard_map/dot_general | solution.py:221
  (221 shorter events, 127.2 us)
Async XLA Ops:
  7.2 22.9 %copy-start.25 = (f32[2,256,256]{2,1,0:T(8,128)S(1)}, f32[2,256,256]{2,1,0:T(8,128)}, u32[]{:S(2)}) copy-start(f32[2,256,256]{2,1,0:T(8,128)} %param.34) | copy-start | bytes 1572868
  7.2 243.2 %all-reduce.3.cloned.1.call-start = ((), (), s32[]{:S(2)}) async-start(), calls=%async_computation | async-start | bytes 4194304 | tf_op jit(solution)/shard_map/psum | solution.py:206
  7.2 22.8 %collective-permute-start.1 = (f32[2,256,256]{2,1,0:T(8,128)}, f32[2,256,256]{2,1,0:T(8,128)S(1)}, u32[]{:S(2)}, u32[]{:S(2)}) collective-permute-start(f32[2,256,256]{2,1,0:T(8,128)} %param.34), channel_id=1, source_target_pairs={{4,0},{8,4},{12,8},{16,12},{20,16},{24,20},{28,24},{5,1},{9,5},{13... | collective-permute-start | bytes 1572872 | tf_op jit(solution)/shard_map/ppermute | solution.py:17
  8.7 21.4 %collective-permute-start = (f32[2,256,256]{2,1,0:T(8,128)}, f32[2,256,256]{2,1,0:T(8,128)S(1)}, u32[]{:S(2)}, u32[]{:S(2)}) collective-permute-start(f32[2,256,256]{2,1,0:T(8,128)} %param.34), channel_id=1, source_target_pairs={{1,0},{2,1},{3,2},{5,4},{6,5},{7,6},{9,8},{10,9},{11,10},{13,12},{... | collective-permute-start | bytes 1572872 | tf_op jit(solution)/shard_map/ppermute | solution.py:17
  10.0 20.0 %collective-permute-start.2 = (f32[2,256,256]{2,1,0:T(8,128)}, f32[2,256,256]{2,1,0:T(8,128)S(1)}, u32[]{:S(2)}, u32[]{:S(2)}) collective-permute-start(f32[2,256,256]{2,1,0:T(8,128)} %param.34), channel_id=1, source_target_pairs={{5,0},{6,1},{7,2},{8,3},{9,4},{10,5},{11,6},{12,7},{13,8},{14,9},{... | collective-permute-start | bytes 1572872 | tf_op jit(solution)/shard_map/ppermute | solution.py:17
  70.2 52.5 %collective-permute-start.3 = (f32[3,256,256]{2,1,0:T(8,128)}, f32[3,256,256]{2,1,0:T(8,128)}, u32[]{:S(2)}, u32[]{:S(2)}) collective-permute-start(f32[3,256,256]{2,1,0:T(8,128)} %get-tuple-element.382), channel_id=1, source_target_pairs={{0,1},{1,2},{2,3},{4,5},{5,6},{6,7},{8,9},{9,10},{10,11},{12,13},{... | collective-permute-start | bytes 2359304 | tf_op jit(solution)/shard_map/ppermute | solution.py:17
  79.7 53.4 %collective-permute-start.5 = (f32[3,256,256]{2,1,0:T(8,128)}, f32[3,256,256]{2,1,0:T(8,128)}, u32[]{:S(2)}, u32[]{:S(2)}) collective-permute-start(f32[3,256,256]{2,1,0:T(8,128)} %get-tuple-element.383), channel_id=1, source_target_pairs={{0,5},{1,6},{2,7},{3,8},{4,9},{5,10},{6,11},{7,12},{8,13},{9,14},{... | collective-permute-start | bytes 2359304 | tf_op jit(solution)/shard_map/ppermute | solution.py:17
  112.7 29.9 %collective-permute-start.4 = (f32[3,256,256]{2,1,0:T(8,128)S(1)}, f32[3,256,256]{2,1,0:T(8,128)}, u32[]{:S(2)}, u32[]{:S(2)}) collective-permute-start(f32[3,256,256]{2,1,0:T(8,128)S(1)} %get-tuple-element.384), channel_id=1, source_target_pairs={{0,4},{4,8},{8,12},{12,16},{16,20},{20,24},{24,28},{1,5},{5,9},{9,... | collective-permute-start | bytes 2359304 | tf_op jit(solution)/shard_map/ppermute | solution.py:17
  116.2 423.4 %all-reduce.5.cloned.1.call-start = ((), (), s32[]{:S(2)}) async-start(), calls=%async_computation.1 | async-start | bytes 4194304 | tf_op jit(solution)/shard_map/psum | solution.py:206
  122.6 21.8 %copy-start.26 = (f32[2,256,256]{2,1,0:T(8,128)S(1)}, f32[2,256,256]{2,1,0:T(8,128)}, u32[]{:S(2)}) copy-start(f32[2,256,256]{2,1,0:T(8,128)} %param.34) | copy-start | bytes 1572868
  144.5 195.6 %copy-start.9 = (f32[2,256,256]{2,1,0:T(8,128)}, f32[2,256,256]{2,1,0:T(8,128)S(1)}, u32[]{:S(2)}) copy-start(f32[2,256,256]{2,1,0:T(8,128)S(1)} %fusion.122) | copy-start | bytes 1572868
  144.5 194.4 %collective-permute-start.8 = (f32[2,256,256]{2,1,0:T(8,128)S(1)}, f32[2,256,256]{2,1,0:T(8,128)}, u32[]{:S(2)}, u32[]{:S(2)}) collective-permute-start(f32[2,256,256]{2,1,0:T(8,128)S(1)} %fusion.122), channel_id=1, source_target_pairs={{5,0},{6,1},{7,2},{8,3},{9,4},{10,5},{11,6},{12,7},{13,8},{14,9},{... | collective-permute-start | bytes 1572872 | tf_op jit(solution)/shard_map/ppermute | solution.py:17
  145.8 194.2 %collective-permute-start.7 = (f32[2,256,256]{2,1,0:T(8,128)S(1)}, f32[2,256,256]{2,1,0:T(8,128)}, u32[]{:S(2)}, u32[]{:S(2)}) collective-permute-start(f32[2,256,256]{2,1,0:T(8,128)S(1)} %fusion.122), channel_id=1, source_target_pairs={{4,0},{8,4},{12,8},{16,12},{20,16},{24,20},{28,24},{5,1},{9,5},{13... | collective-permute-start | bytes 1572872 | tf_op jit(solution)/shard_map/ppermute | solution.py:17
  147.1 193.0 %collective-permute-start.6 = (f32[2,256,256]{2,1,0:T(8,128)S(1)}, f32[2,256,256]{2,1,0:T(8,128)}, u32[]{:S(2)}, u32[]{:S(2)}) collective-permute-start(f32[2,256,256]{2,1,0:T(8,128)S(1)} %fusion.122), channel_id=1, source_target_pairs={{1,0},{2,1},{3,2},{5,4},{6,5},{7,6},{9,8},{10,9},{11,10},{13,12},{... | collective-permute-start | bytes 1572872 | tf_op jit(solution)/shard_map/ppermute | solution.py:17
  316.0 10.0 %copy-start.34 = (f32[1,2,512,256]{3,1,2,0:T(2,128)S(1)}, f32[1,2,512,256]{3,1,2,0:T(2,128)}, u32[]{:S(2)}) copy-start(f32[1,2,512,256]{3,1,2,0:T(2,128)} %copy.26) | copy-start | bytes 3145732
  378.0 36.2 %copy-start.27 = (f32[1,2,65536]{2,1,0:T(2,128)S(1)}, f32[1,2,65536]{2,1,0:T(2,128)}, u32[]{:S(2)}) copy-start(f32[1,2,65536]{2,1,0:T(2,128)} %get-tuple-element.397) | copy-start | bytes 1572868
  378.0 36.2 %copy-start.28 = (f32[1,2,65536]{2,1,0:T(2,128)S(1)}, f32[1,2,65536]{2,1,0:T(2,128)}, u32[]{:S(2)}) copy-start(f32[1,2,65536]{2,1,0:T(2,128)} %get-tuple-element.395) | copy-start | bytes 1572868
  378.0 36.2 %copy-start.29 = (f32[1,2,65536]{2,1,0:T(2,128)S(1)}, f32[1,2,65536]{2,1,0:T(2,128)}, u32[]{:S(2)}) copy-start(f32[1,2,65536]{2,1,0:T(2,128)} %get-tuple-element.399) | copy-start | bytes 1572868
  378.0 36.2 %copy-start.30 = (f32[1,2,65536]{2,1,0:T(2,128)S(1)}, f32[1,2,65536]{2,1,0:T(2,128)}, u32[]{:S(2)}) copy-start(f32[1,2,65536]{2,1,0:T(2,128)} %get-tuple-element.393) | copy-start | bytes 1572868
  380.0 39.5 %collective-permute-start.9 = (f32[3,256,256]{2,1,0:T(8,128)S(1)}, f32[3,256,256]{2,1,0:T(8,128)S(1)}, u32[]{:S(2)}, u32[]{:S(2)}) collective-permute-start(f32[3,256,256]{2,1,0:T(8,128)S(1)} %get-tuple-element.379), channel_id=1, source_target_pairs={{0,1},{1,2},{2,3},{4,5},{5,6},{6,7},{8,9},{9,10},{10,11},{12,13},{... | collective-permute-start | bytes 2359304 | tf_op jit(solution)/shard_map/ppermute | solution.py:17
  381.3 49.7 %collective-permute-start.11 = (f32[3,256,256]{2,1,0:T(8,128)S(1)}, f32[3,256,256]{2,1,0:T(8,128)S(1)}, u32[]{:S(2)}, u32[]{:S(2)}) collective-permute-start(f32[3,256,256]{2,1,0:T(8,128)S(1)} %get-tuple-element.380), channel_id=1, source_target_pairs={{0,5},{1,6},{2,7},{3,8},{4,9},{5,10},{6,11},{7,12},{8,13},{9,14},{... | collective-permute-start | bytes 2359304 | tf_op jit(solution)/shard_map/ppermute | solution.py:17
  412.4 29.5 %collective-permute-start.10 = (f32[3,256,256]{2,1,0:T(8,128)S(1)}, f32[3,256,256]{2,1,0:T(8,128)S(1)}, u32[]{:S(2)}, u32[]{:S(2)}) collective-permute-start(f32[3,256,256]{2,1,0:T(8,128)S(1)} %get-tuple-element.381), channel_id=1, source_target_pairs={{0,4},{4,8},{8,12},{12,16},{16,20},{20,24},{24,28},{1,5},{5,9},{9,... | collective-permute-start | bytes 2359304 | tf_op jit(solution)/shard_map/ppermute | solution.py:17
  419.4 23.9 %copy-start.10 = (f32[2,256,256]{2,1,0:T(8,128)S(1)}, f32[2,256,256]{2,1,0:T(8,128)}, u32[]{:S(2)}) copy-start(f32[2,256,256]{2,1,0:T(8,128)} %copy-done.9) | copy-start | bytes 1572868
  443.2 96.4 %copy-start.6 = (f32[1,1,256,256]{3,2,1,0:T(8,128)S(1)}, f32[1,1,256,256]{3,2,1,0:T(8,128)}, u32[]{:S(2)}) copy-start(f32[1,1,256,256]{3,2,1,0:T(8,128)} %copy-done.5) | copy-start | bytes 786436
  443.2 96.3 %copy-start.8 = (f32[1,1,256,256]{3,2,1,0:T(8,128)S(1)}, f32[1,1,256,256]{3,2,1,0:T(8,128)}, u32[]{:S(2)}) copy-start(f32[1,1,256,256]{3,2,1,0:T(8,128)} %copy-done.7) | copy-start | bytes 786436
  443.2 96.3 %copy-start.12 = (f32[1,1,256,256]{3,2,1,0:T(8,128)S(1)}, f32[1,1,256,256]{3,2,1,0:T(8,128)}, u32[]{:S(2)}) copy-start(f32[1,1,256,256]{3,2,1,0:T(8,128)} %copy-done.11) | copy-start | bytes 786436
  443.2 96.3 %copy-start.14 = (f32[1,1,256,256]{3,2,1,0:T(8,128)S(1)}, f32[1,1,256,256]{3,2,1,0:T(8,128)}, u32[]{:S(2)}) copy-start(f32[1,1,256,256]{3,2,1,0:T(8,128)} %copy-done.13) | copy-start | bytes 786436
  443.3 96.3 %copy-start.16 = (f32[1,1,256,256]{3,2,1,0:T(8,128)S(1)}, f32[1,1,256,256]{3,2,1,0:T(8,128)}, u32[]{:S(2)}) copy-start(f32[1,1,256,256]{3,2,1,0:T(8,128)} %copy-done.15) | copy-start | bytes 786436
  443.3 96.3 %copy-start.18 = (f32[1,1,256,256]{3,2,1,0:T(8,128)S(1)}, f32[1,1,256,256]{3,2,1,0:T(8,128)}, u32[]{:S(2)}) copy-start(f32[1,1,256,256]{3,2,1,0:T(8,128)} %copy-done.17) | copy-start | bytes 786436
  443.3 96.3 %copy-start.20 = (f32[1,1,256,256]{3,2,1,0:T(8,128)S(1)}, f32[1,1,256,256]{3,2,1,0:T(8,128)}, u32[]{:S(2)}) copy-start(f32[1,1,256,256]{3,2,1,0:T(8,128)} %copy-done.19) | copy-start | bytes 786436
  443.3 96.3 %copy-start.22 = (f32[1,1,256,256]{3,2,1,0:T(8,128)S(1)}, f32[1,1,256,256]{3,2,1,0:T(8,128)}, u32[]{:S(2)}) copy-start(f32[1,1,256,256]{3,2,1,0:T(8,128)} %copy-done.21) | copy-start | bytes 786436
  598.4 11.0 %copy-start.33 = (f32[1,2,512,256]{3,1,2,0:T(2,128)S(1)}, f32[1,2,512,256]{3,1,2,0:T(2,128)}, u32[]{:S(2)}) copy-start(f32[1,2,512,256]{3,1,2,0:T(2,128)} %copy.27) | copy-start | bytes 3145732
  (22 other events, 59.0 us)
Sparse Core Ops, SparseCore 0:
  116.3 134.0 all-reduce.2
  378.1 161.4 all-reduce.4
where the time goes:
time: 639 us; the launch traced here: 628 us
  waiting for transfers between devices  255 us (40%)
  matrix products  98.5 us (15%)
  starting transfers between devices  88.1 us (14%)
  local copies, waits for them, and re-layouts  82.6 us (13%)
  other arithmetic  56.9 us (9%)
  between operations  36.9 us (6%)
  loops' own time  10.7 us (2%)
    psum x2, waiting for transfers between devices, on_device(): summed = lax.psum(mode_terms, ('scan', 'col'))  197 us
    ppermute x12, starting transfers between devices, from_behind(): return lax.ppermute(shard, axis, pairs)  88.1 us
    ppermute x12, waiting for transfers between devices, from_behind(): return lax.ppermute(shard, axis, pairs)  57.3 us
    dot_general x2, matrix products, on_device(): jnp.dot(probe_modes.reshape(mode_count, 2 * pixels), ortho_flat.T, precis...  21 us
    dot_general x2, matrix products, on_device(): jnp.dot(stashed.reshape(frames, 2 * pixels), ortho_flat.T, precision=high...  19.3 us
    dynamic_update_slice x2, local copies, waits for them, and re-layouts, visit(): lax.dynamic_update_slice(totals, window + update, (anchor, offset[0], off...  18.8 us
    unnamed x91, local copies, waits for them, and re-layouts  16.5 us
    another operation x12, other arithmetic, orthonormal(): return jnp.stack([jnp.stack([pair[0], pair[1]]) for pair in columns])  14 us
  transfers between devices with their start and end apart: 14, of which 7 were waited for; matrix products, arithmetic and copies ran while one was open for 16% of the time, Pallas kernels for 0%

commit v1 on v0

v1 whole, which is shorter than its diff:
```python
import math

import jax
import jax.numpy as jnp
from jax import lax
from jax.experimental import pallas as pl
from jax.experimental.pallas import tpu as pltpu
from jax.sharding import PartitionSpec as P

ITERS = 2

VMEM = pl.BlockSpec(memory_space=pltpu.VMEM)
SMEM = pl.BlockSpec(memory_space=pltpu.SMEM)


def from_behind(shard, axis, by):
    size = lax.axis_size(axis)
    pairs = [(i, i + by) for i in range(size) if 0 <= i + by < size]
    return lax.ppermute(shard, axis, pairs)


def make_tables(length):
    indices = jnp.arange(length, dtype=jnp.int32)
    phases = indices[:, None] * indices[None, :] % length
    angles = phases.astype(jnp.float32) * (2.0 * math.pi / length)
    factor = 1.0 / math.sqrt(length)
    cosine = jnp.cos(angles) * factor
    sine_table = jnp.sin(angles) * factor
    rows_table = jnp.concatenate(
        [jnp.concatenate([cosine, sine_table], 1), jnp.concatenate([-sine_table, cosine], 1)], 0
    )
    cols_table = jnp.concatenate(
        [jnp.concatenate([cosine, -sine_table], 1), jnp.concatenate([sine_table, cosine], 1)], 0
    )
    return (rows_table.astype(jnp.bfloat16), cols_table.astype(jnp.bfloat16))


def apply_transform(stacked, first_table, second_table):
    length = stacked.shape[1]
    halfway = jnp.dot(first_table, stacked, preferred_element_type=jnp.float32).astype(jnp.bfloat16)
    beside = jnp.concatenate([halfway[:length], halfway[length:]], 1)
    return jnp.dot(beside, second_table, preferred_element_type=jnp.float32)


def frames_kernel(
    count, offsets, weights, home, beyond, lower, corner, amplitudes, modes, rows_table, cols_table,
    totals, mode_terms, stashed, wide,
):
    length = amplitudes.shape[1]
    block_height, block_width = home.shape[1:]
    mode_count = modes.shape[0] // 2
    wide[:, :block_height, :block_width] = home[...]
    wide[:, :block_height, block_width:] = beyond[...]
    wide[:, block_height:, :block_width] = lower[...]
    wide[:, block_height:, block_width:] = corner[...]
    totals[...] = jnp.zeros_like(totals)
    mode_terms[...] = jnp.zeros_like(mode_terms)
    stashed[...] = jnp.zeros_like(stashed)
    full_width = block_width + length

    def visit(slot, carry):
        row, col = offsets[slot, 0], offsets[slot, 1]
        start = pl.multiple_of(row // 8 * 8, 8)
        rest = row - start
        rows = pl.ds(start, length + 8)

        def cut(plane):
            band = wide[plane, rows, :]
            band = pltpu.roll(band, lax.rem(full_width - col, full_width), 1)[:, :length]
            return pltpu.roll(band, lax.rem(length + 8 - rest, length + 8), 0)[:length]

        def place(plane, piece):
            band = jnp.concatenate([piece, jnp.zeros((8, length), jnp.float32)], 0)
            band = pltpu.roll(band, rest, 0)
            band = jnp.concatenate([band, jnp.zeros((length + 8, block_width), jnp.float32)], 1)
            totals[plane, rows, :] += pltpu.roll(band, col, 1)

        object_real = cut(0)
        object_imag = cut(1)
        probe_real = weights[slot, 0] * modes[0]
        probe_imag = weights[slot, 0] * modes[1]
        for k in range(1, mode_count):
            probe_real += weights[slot, k] * modes[2 * k]
            probe_imag += weights[slot, k] * modes[2 * k + 1]
        place(2, probe_real * probe_real + probe_imag * probe_imag)
        exit_real = probe_real * object_real - probe_imag * object_imag
        exit_imag = probe_real * object_imag + probe_imag * object_real
        stacked = jnp.concatenate([exit_real, exit_imag], 0).astype(jnp.bfloat16)
        far = apply_transform(stacked, rows_table[...], cols_table[...])
        far_real, far_imag = far[:, :length], far[:, length:]
        magnitude = jnp.sqrt(far_real * far_real + far_imag * far_imag)
        factor = amplitudes[slot].astype(jnp.float32) / jnp.maximum(magnitude, 0.5)
        scaled = jnp.concatenate([far_real * factor, far_imag * factor], 0).astype(jnp.bfloat16)
        back = apply_transform(scaled, cols_table[...], rows_table[...])
        diff_real = back[:, :length] - exit_real
        diff_imag = back[:, length:] - exit_imag
        place(0, probe_real * diff_real + probe_imag * diff_imag)
        place(1, probe_real * diff_imag - probe_imag * diff_real)
        step_real = object_real * diff_real + object_imag * diff_imag
        step_imag = object_real * diff_imag - object_imag * diff_real
        stashed[slot, 0] = step_real
        stashed[slot, 1] = step_imag
        for k in range(mode_count):
            mode_terms[2 * k] += weights[slot, k] * step_real
            mode_terms[2 * k + 1] += weights[slot, k] * step_imag
        return carry

    lax.fori_loop(0, count[0], visit, 0)


def refit_kernel(root_total, count, weights, summed, modes, stashed, new_modes, new_weights, lifted):
    planes, length = modes.shape[:2]
    mode_count = planes // 2
    frames = stashed.shape[0]
    pixels = float(length * length)
    height = 8
    steps = length // height
    pairs = [(i, j) for j in range(mode_count) for i in range(j + 1)]
    strict = [(i, j) for i, j in pairs if i < j]

    def fold(value):
        total = value[:, :128]
        for at in range(128, length, 128):
            total = total + value[:, at:at + 128]
        return total

    def at_rows(step):
        return pl.ds(pl.multiple_of(step * height, height), height)

    def gram_step(step, sums):
        rows = at_rows(step)
        raised = []
        for p in range(planes):
            value = modes[p, rows, :] + summed[p, rows, :] / root_total
            lifted[p, rows, :] = value
            raised.append(value)
        real, imag = raised[0::2], raised[1::2]
        terms = [fold(real[i] * real[j] + imag[i] * imag[j]) for i, j in pairs]
        terms += [fold(real[i] * imag[j] - imag[i] * real[j]) for i, j in strict]
        return tuple(a + b for a, b in zip(sums, terms))

    blank = jnp.zeros((height, 128), jnp.float32)
    sums = lax.fori_loop(0, steps, gram_step, (blank,) * (len(pairs) + len(strict)))

    def whole(value):
        return jnp.sum(jnp.sum(value, 0, keepdims=True), 1, keepdims=True)

    gram_real = {p: whole(s) / pixels for p, s in zip(pairs, sums)}
    gram_imag = {p: whole(s) / pixels for p, s in zip(strict, sums[len(pairs):])}
    upper_real, upper_imag = {}, {}
    for j in range(mode_count):
        for i in range(j):
            sum_real, sum_imag = gram_real[i, j], gram_imag[i, j]
            for k in range(i):
                a, b, c, d = upper_real[k, i], upper_imag[k, i], upper_real[k, j], upper_imag[k, j]
                sum_real = sum_real - (a * c + b * d)
                sum_imag = sum_imag - (a * d - b * c)
            upper_real[i, j] = sum_real / upper_real[i, i]
            upper_imag[i, j] = sum_imag / upper_real[i, i]
        diagonal = gram_real[j, j]
        for k in range(j):
            diagonal = diagonal - (upper_real[k, j] * upper_real[k, j] + upper_imag[k, j] * upper_imag[k, j])
        upper_real[j, j] = jnp.sqrt(diagonal)
    wide = {p: jnp.broadcast_to(v, (height, length)) for p, v in upper_real.items()}
    wide_imag = {p: jnp.broadcast_to(v, (height, length)) for p, v in upper_imag.items()}
    inverse = {j: jnp.broadcast_to(1.0 / upper_real[j, j], (height, length)) for j in range(mode_count)}

    def basis_step(step, carry):
        rows = at_rows(step)
        basis = []
        for j in range(mode_count):
            real, imag = lifted[2 * j, rows, :], lifted[2 * j + 1, rows, :]
            for i in range(j):
                a, b = wide[i, j], wide_imag[i, j]
                c, d = basis[i]
                real = real - (a * c - b * d)
                imag = imag - (a * d + b * c)
            real, imag = real * inverse[j], imag * inverse[j]
            basis.append((real, imag))
            new_modes[2 * j, rows, :] = real
            new_modes[2 * j + 1, rows, :] = imag
        return carry

    lax.fori_loop(0, steps, basis_step, 0)

    def fit_step(step, sums):
        rows = at_rows(step)
        basis = [new_modes[p, rows, :] for p in range(planes)]
        terms = []
        for j in range(mode_count):
            real, imag = modes[2 * j, rows, :], modes[2 * j + 1, rows, :]
            terms += [fold(basis[2 * k] * real + basis[2 * k + 1] * imag) for k in range(mode_count)]
        for g in range(frames):
            real, imag = stashed[g, 0, rows, :], stashed[g, 1, rows, :]
            terms += [fold(basis[2 * k] * real + basis[2 * k + 1] * imag) for k in range(mode_count)]
        return tuple(a + b for a, b in zip(sums, terms))

    sums = lax.fori_loop(0, steps, fit_step, (blank,) * (mode_count * (mode_count + frames)))
    sums = [whole(s) / pixels for s in sums]
    for g in range(frames):
        for k in range(mode_count):
            refit = 0.5 * sums[mode_count * (mode_count + g) + k]
            for j in range(mode_count):
                refit = refit + weights[g, j] * sums[mode_count * j + k]
            kept = jnp.full((1, 1), weights[g, k], jnp.float32)
            new_weights[g:g + 1, k:k + 1] = jnp.where(g < count[0], refit, kept)


def settle(totals, block_height, block_width, length, col_index, col_count):
    arrived = from_behind(totals[:, :block_height, block_width:], "col", 1)
    lowered = from_behind(totals[:, block_height:, :block_width], "scan", 1)
    corner = from_behind(totals[:, block_height:, block_width:], ("scan", "col"), col_count + 1)
    corner = jnp.where(col_index > 0, corner, jnp.zeros_like(corner))
    settled = totals[:, :block_height, :block_width]
    settled = settled.at[:, :, :length].add(arrived)
    settled = settled.at[:, :length, :].add(lowered)
    settled = settled.at[:, :length, :length].add(corner)
    return settled


def shape(*dims):
    return jax.ShapeDtypeStruct(dims, jnp.float32)


def on_device(object_field, amplitudes, positions, frame_count, coefficients, probe_modes):
    frames, length = amplitudes.shape[:2]
    mode_count = probe_modes.shape[0]
    planes = 2 * mode_count
    block_height, block_width = object_field.shape[1:]
    scan_count = lax.axis_size("scan")
    col_count = lax.axis_size("col")
    col_index = lax.axis_index("col")
    block_corner = jnp.stack([lax.axis_index("scan") * block_height, col_index * block_width])
    offsets = positions - block_corner[None, :]
    root_total = math.sqrt(frames * scan_count * col_count)
    rows_table, cols_table = make_tables(length)
    modes = probe_modes.reshape(planes, length, length)
    for iteration in range(ITERS):
        lower_rim = from_behind(object_field, "scan", -1)
        beyond = from_behind(object_field, "col", -1)
        corner = from_behind(object_field, ("scan", "col"), -(col_count + 1))
        totals, mode_terms, stashed = pl.pallas_call(
            frames_kernel,
            name="frames",
            out_shape=(
                shape(3, block_height + length, block_width + length),
                shape(planes, length, length),
                shape(frames, 2, length, length),
            ),
            in_specs=[SMEM] * 3 + [VMEM] * 8,
            out_specs=(VMEM,) * 3,
            scratch_shapes=[pltpu.VMEM((2, block_height + length, block_width + length), jnp.float32)],
            cost_estimate=pl.CostEstimate(flops=2 * 10**9, bytes_accessed=10**7, transcendentals=0),
        )(
            frame_count, offsets, coefficients, object_field, beyond, lower_rim, corner, amplitudes,
            modes, rows_table, cols_table,
        )
        summed = lax.psum(mode_terms, ("scan", "col"))
        settled = settle(totals, block_height, block_width, length, col_index, col_count)
        object_field = object_field + settled[:2] / (settled[2] + 1.0)
        modes, coefficients = pl.pallas_call(
            lambda *refs: refit_kernel(root_total, *refs),
            name="refit",
            out_shape=(shape(planes, length, length), shape(frames, mode_count)),
            in_specs=[SMEM] * 2 + [VMEM] * 3,
            out_specs=(VMEM,) * 2,
            scratch_shapes=[pltpu.VMEM((planes, length, length), jnp.float32)],
        )(frame_count, coefficients, summed, modes, stashed)
    return (object_field, modes.reshape(probe_modes.shape), coefficients)


def solution(mesh):
    placed = (
        P(None, "scan", "col"),
        P(("scan", "col"), None, None),
        P(("scan", "col"), None),
        P(("scan", "col")),
        P(("scan", "col"), None),
        P(),
    )
    return jax.shard_map(
        on_device,
        mesh=mesh,
        in_specs=placed,
        out_specs=(P(None, "scan", "col"), P(), P(("scan", "col"), None)),
        check_vma=False,
    )
```

time: 639 us -> 374 us (0.59); the launches traced: 628 us -> 374 us
  matrix products: 98.5 us -> 0 us
  local copies, waits for them, and re-layouts: 82.6 us -> 5.84 us
  other arithmetic: 56.9 us -> 8.86 us
  starting transfers between devices: 88.1 us -> 40.9 us
  Pallas kernels: 0 us -> 31.2 us
  between operations: 36.9 us -> 14.9 us
  waiting for transfers between devices: 255 us -> 272 us
  loops' own time: 10.7 us -> 0 us
    dot_general x24 -> x0, matrix products: 98.5 us -> none  [the longest x2 21 us: on_device(): jnp.dot(probe_modes.reshape(mode_count, 2 * pixels), ortho_flat.T, precis...]
    ppermute x12, starting transfers between devices: 88.1 us -> 40.8 us  [from_behind(): return lax.ppermute(shard, axis, pairs)]
    pallas_call x0 -> x4, Pallas kernels: none -> 31.2 us  [the longest x2 17.5 us: on_device(): pl.pallas_call(frames_kernel, name='frames', out_shape=(shape(3, block_he...]
    ppermute x12, waiting for transfers between devices: 57.3 us -> 76.6 us  [from_behind(): return lax.ppermute(shard, axis, pairs)]
    dynamic_update_slice x2 -> x0, local copies, waits for them, and re-layouts: 18.8 us -> none  [visit(): lax.dynamic_update_slice(totals, window + update, (anchor, offset[0], off...]
    slice x14 -> x0, local copies, waits for them, and re-layouts: 16 us -> none  [the longest x2 8.7 us: orthonormal(): vector_real = flat_modes[right_index, 0]]
    another operation x20 -> x2, other arithmetic: 17.2 us -> 2.1 us  [the longest x12 14 us: orthonormal(): return jnp.stack([jnp.stack([pair[0], pair[1]]) for pair in columns])]
    unnamed x91 -> x18, local copies, waits for them, and re-layouts: 16.5 us -> 2.11 us
  transfers between devices with their start and end apart: 14 -> 14, of which waited for: 7 -> 8; matrix products, arithmetic and copies ran while one was open for 16% -> 2% of each run, Pallas kernels for 0% -> 2%
where the time goes in v1:
time: 374 us
  waiting for transfers between devices  272 us (73%)
  starting transfers between devices  40.9 us (11%)
  Pallas kernels  31.2 us (8%)
  between operations  14.9 us (4%)
  other arithmetic  8.86 us (2%)
  local copies, waits for them, and re-layouts  5.84 us (2%)
    psum x2, waiting for transfers between devices, on_device(): summed = lax.psum(mode_terms, ('scan', 'col'))  195 us
    ppermute x12, waiting for transfers between devices, from_behind(): return lax.ppermute(shard, axis, pairs)  76.6 us
    ppermute x12, starting transfers between devices, from_behind(): return lax.ppermute(shard, axis, pairs)  40.8 us
    pallas_call x2, Pallas kernels, on_device(): pl.pallas_call(frames_kernel, name='frames', out_shape=(shape(3, block_he...  17.5 us
    pallas_call x2, Pallas kernels, on_device(): pl.pallas_call(lambda *refs: refit_kernel(root_total, *refs), name='refit...  13.7 us
  transfers between devices with their start and end apart: 14, of which 8 were waited for; matrix products, arithmetic and copies ran while one was open for 2% of the time, Pallas kernels for 2%

profile of v1, /device:TPU:0, one launch (start us, length us, event | category | flops | bytes accessed | tf_op | source)
XLA Modules:
  0.0 373.6 jit_solution(7366263010557019900)
XLA Ops:
  7.2 1.3 collective-permute-start.2
  8.5 1.3 collective-permute-start.1
  9.8 1.3 collective-permute-start
  11.1 1.0 fusion.12
  12.8 1.1 negate_convert_fusion
  14.0 1.1 fusion.1
  15.1 1.2 broadcast_subtract_fusion.offsets
  16.3 5.7 %collective-permute-done.2.corner = f32[2,256,256]{2,1,0:T(8,128)S(1)} collective-permute-done((f32[2,256,256]{2,1,0:T(8,128)}, f32[2,256,256]{2,1,0:T(8,128)S(1)}, u32[]{:S(2)}, u32[]{:S(2)}) %collective-permute-start.2) | collective-permute-done | bytes 524320 | tf_op jit(solution)/shard_map/ppermute | solution.py:19
  22.1 4.3 %collective-permute-done.1.lower = f32[2,256,256]{2,1,0:T(8,128)S(1)} collective-permute-done((f32[2,256,256]{2,1,0:T(8,128)}, f32[2,256,256]{2,1,0:T(8,128)S(1)}, u32[]{:S(2)}, u32[]{:S(2)}) %collective-permute-start.1) | collective-permute-done | bytes 524320 | tf_op jit(solution)/shard_map/ppermute | solution.py:19
  27.3 8.7 %frames.2 = (f32[3,512,512]{2,1,0:T(8,128)}, f32[8,256,256]{2,1,0:T(8,128)}, f32[2,2,256,256]{3,2,1,0:T(8,128)}) custom-call(s32[1]{0:T(128)S(6)} %copy.11.count.refs_0_, s32[2,2]{1,0:T(2,128)} %broadcast_subtract_fusion.offsets, f32[2,4]{1,0:T(2,128)} %refs_1_.1, f32[2,256,256]{2,1,0:T(8,128)} %home.1, f32[2,256,256]{2,1,0:T(8,128)} %copy-done.5, ...), custom_call_target="tpu_custom_call" | custom-call | flops 2000000000 | bytes 10000000 | tf_op jit(solution)/shard_map/frames/pallas_call | solution.py:242
  36.0 1.9 fusion.14
  37.9 5.2 %collective-permute-start.3 = (f32[3,256,256]{2,1,0:T(8,128)S(1)}, f32[3,256,256]{2,1,0:T(8,128)S(1)}, u32[]{:S(2)}, u32[]{:S(2)}) collective-permute-start(f32[3,256,256]{2,1,0:T(8,128)S(1)} %get-tuple-element.146), channel_id=1, source_target_pairs={{0,1},{1,2},{2,3},{4,5},{5,6},{6,7},{8,9},{9,10},{10,11},{12,13},{... | collective-permute-start | bytes 2359304 | tf_op jit(solution)/shard_map/ppermute | solution.py:19
  43.2 12.9 %collective-permute-start.5 = (f32[3,256,256]{2,1,0:T(8,128)S(1)}, f32[3,256,256]{2,1,0:T(8,128)}, u32[]{:S(2)}, u32[]{:S(2)}) collective-permute-start(f32[3,256,256]{2,1,0:T(8,128)S(1)} %get-tuple-element.147), channel_id=1, source_target_pairs={{0,5},{1,6},{2,7},{3,8},{4,9},{5,10},{6,11},{7,12},{8,13},{9,14},{... | collective-permute-start | bytes 2359304 | tf_op jit(solution)/shard_map/ppermute | solution.py:19
  56.1 3.5 collective-permute-start.4
  59.7 17.6 %collective-permute-done.5 = f32[3,256,256]{2,1,0:T(8,128)} collective-permute-done((f32[3,256,256]{2,1,0:T(8,128)S(1)}, f32[3,256,256]{2,1,0:T(8,128)}, u32[]{:S(2)}, u32[]{:S(2)}) %collective-permute-start.5) | collective-permute-done | bytes 786464 | tf_op jit(solution)/shard_map/ppermute | solution.py:19
  77.3 16.1 %collective-permute-done.4 = f32[3,256,256]{2,1,0:T(8,128)} collective-permute-done((f32[3,256,256]{2,1,0:T(8,128)S(1)}, f32[3,256,256]{2,1,0:T(8,128)}, u32[]{:S(2)}, u32[]{:S(2)}) %collective-permute-start.4) | collective-permute-done | bytes 786464 | tf_op jit(solution)/shard_map/ppermute | solution.py:19
  93.4 1.7 select_add_fusion.1
  95.2 1.3 collective-permute-start.8
  96.5 1.3 collective-permute-start.7
  97.8 1.3 collective-permute-start.6
  99.1 96.3 %all-reduce.3.cloned.1.call-done.refs_2_ = f32[8,256,256]{2,1,0:T(8,128)} async-done(((f32[8,256,256]{2,1,0:T(8,128)}), f32[8,256,256]{2,1,0:T(8,128)}) %all-reduce.3.cloned.1.call-update) | async-done | bytes 2097168 | tf_op jit(solution)/shard_map/psum | solution.py:258
  195.4 6.9 %refit.2 = (f32[8,256,256]{2,1,0:T(8,128)}, f32[2,4]{1,0:T(2,128)}) custom-call(s32[1]{0:T(128)S(6)} %copy.11.count.refs_0_, f32[2,4]{1,0:T(2,128)} %refs_1_.1, f32[8,256,256]{2,1,0:T(8,128)} %all-reduce.3.cloned.1.call-done.refs_2_, f32[8,256,256]{2,1,0:T(8,128)} %bitcast.9, f32[2,2,256,256]{3,2,1,0:T(8,128)} %get-tuple-element.135.refs_4_), custom_call_target="tpu_custom_call" | custom-call | tf_op jit(solution)/shard_map/refit/pallas_call | solution.py:261
  203.5 8.8 %frames.3 = (f32[3,512,512]{2,1,0:T(8,128)}, f32[8,256,256]{2,1,0:T(8,128)}, f32[2,2,256,256]{3,2,1,0:T(8,128)}) custom-call(s32[1]{0:T(128)S(6)} %copy.11.count.refs_0_, s32[2,2]{1,0:T(2,128)} %broadcast_subtract_fusion.offsets, f32[2,4]{1,0:T(2,128)} %get-tuple-element.136.weights.refs_1_, f32[2,256,256]{2,1,0:T(8,128)} %copy-done, ...), custom_call_target="tpu_custom_call" | custom-call | flops 2000000000 | bytes 10000000 | tf_op jit(solution)/shard_map/frames/pallas_call | solution.py:242
  212.3 1.9 fusion.13
  214.1 1.3 collective-permute-start.9
  215.5 5.8 %collective-permute-start.11 = (f32[3,256,256]{2,1,0:T(8,128)S(1)}, f32[3,256,256]{2,1,0:T(8,128)}, u32[]{:S(2)}, u32[]{:S(2)}) collective-permute-start(f32[3,256,256]{2,1,0:T(8,128)S(1)} %get-tuple-element.144), channel_id=1, source_target_pairs={{0,5},{1,6},{2,7},{3,8},{4,9},{5,10},{6,11},{7,12},{8,13},{9,14},{... | collective-permute-start | bytes 2359304 | tf_op jit(solution)/shard_map/ppermute | solution.py:19
  221.3 4.3 %collective-permute-start.10 = (f32[3,256,256]{2,1,0:T(8,128)S(1)}, f32[3,256,256]{2,1,0:T(8,128)}, u32[]{:S(2)}, u32[]{:S(2)}) collective-permute-start(f32[3,256,256]{2,1,0:T(8,128)S(1)} %get-tuple-element.145), channel_id=1, source_target_pairs={{0,4},{4,8},{8,12},{12,16},{16,20},{20,24},{24,28},{1,5},{5,9},{9,... | collective-permute-start | bytes 2359304 | tf_op jit(solution)/shard_map/ppermute | solution.py:19
  225.6 16.8 %collective-permute-done.11 = f32[3,256,256]{2,1,0:T(8,128)} collective-permute-done((f32[3,256,256]{2,1,0:T(8,128)S(1)}, f32[3,256,256]{2,1,0:T(8,128)}, u32[]{:S(2)}, u32[]{:S(2)}) %collective-permute-start.11) | collective-permute-done | bytes 786464 | tf_op jit(solution)/shard_map/ppermute | solution.py:19
  242.4 16.0 %collective-permute-done.10 = f32[3,256,256]{2,1,0:T(8,128)} collective-permute-done((f32[3,256,256]{2,1,0:T(8,128)S(1)}, f32[3,256,256]{2,1,0:T(8,128)}, u32[]{:S(2)}, u32[]{:S(2)}) %collective-permute-start.10) | collective-permute-done | bytes 786464 | tf_op jit(solution)/shard_map/ppermute | solution.py:19
  258.4 1.7 select_add_fusion
  261.0 98.9 %all-reduce.5.cloned.1.call-done.refs_2_ = f32[8,256,256]{2,1,0:T(8,128)} async-done(((f32[8,256,256]{2,1,0:T(8,128)}), f32[8,256,256]{2,1,0:T(8,128)}) %all-reduce.5.cloned.1.call-update) | async-done | bytes 2097168 | tf_op jit(solution)/shard_map/psum | solution.py:258
  360.0 6.8 %refit.3 = (f32[8,256,256]{2,1,0:T(8,128)}, f32[2,4]{1,0:T(2,128)}) custom-call(s32[1]{0:T(128)S(6)} %copy.11.count.refs_0_, f32[2,4]{1,0:T(2,128)} %get-tuple-element.136.weights.refs_1_, f32[8,256,256]{2,1,0:T(8,128)} %all-reduce.5.cloned.1.call-done.refs_2_, f32[8,256,256]{2,1,0:T(8,128)} %get-tuple-element.137.modes.refs_3_, ...), custom_call_target="tpu_custom_call" | custom-call | tf_op jit(solution)/shard_map/refit/pallas_call | solution.py:261
  (33 shorter events, 3.3 us)
Async XLA Ops:
  7.2 188.3 %all-reduce.3.cloned.1.call-start = ((), (), s32[]{:S(2)}) async-start(), calls=%async_computation | async-start | bytes 4194304 | tf_op jit(solution)/shard_map/psum | solution.py:258
  7.2 14.8 %collective-permute-start.2 = (f32[2,256,256]{2,1,0:T(8,128)}, f32[2,256,256]{2,1,0:T(8,128)S(1)}, u32[]{:S(2)}, u32[]{:S(2)}) collective-permute-start(f32[2,256,256]{2,1,0:T(8,128)} %home.1), channel_id=1, source_target_pairs={{5,0},{6,1},{7,2},{8,3},{9,4},{10,5},{11,6},{12,7},{13,8},{14,9},{... | collective-permute-start | bytes 1572872 | tf_op jit(solution)/shard_map/ppermute | solution.py:19
  8.5 17.9 %collective-permute-start.1 = (f32[2,256,256]{2,1,0:T(8,128)}, f32[2,256,256]{2,1,0:T(8,128)S(1)}, u32[]{:S(2)}, u32[]{:S(2)}) collective-permute-start(f32[2,256,256]{2,1,0:T(8,128)} %home.1), channel_id=1, source_target_pairs={{4,0},{8,4},{12,8},{16,12},{20,16},{24,20},{28,24},{5,1},{9,5},{13... | collective-permute-start | bytes 1572872 | tf_op jit(solution)/shard_map/ppermute | solution.py:19
  9.8 16.6 %collective-permute-start = (f32[2,256,256]{2,1,0:T(8,128)}, f32[2,256,256]{2,1,0:T(8,128)S(1)}, u32[]{:S(2)}, u32[]{:S(2)}) collective-permute-start(f32[2,256,256]{2,1,0:T(8,128)} %home.1), channel_id=1, source_target_pairs={{1,0},{2,1},{3,2},{5,4},{6,5},{7,6},{9,8},{10,9},{11,10},{13,12},{... | collective-permute-start | bytes 1572872 | tf_op jit(solution)/shard_map/ppermute | solution.py:19
  22.1 4.3 %copy-start.3 = (f32[2,256,256]{2,1,0:T(8,128)}, f32[2,256,256]{2,1,0:T(8,128)S(1)}, u32[]{:S(2)}) copy-start(f32[2,256,256]{2,1,0:T(8,128)S(1)} %collective-permute-done.2.corner) | copy-start | bytes 1572868
  26.4 0.8 copy-start.4
  26.4 1.0 copy-start.5
  37.9 21.8 %collective-permute-start.3 = (f32[3,256,256]{2,1,0:T(8,128)S(1)}, f32[3,256,256]{2,1,0:T(8,128)S(1)}, u32[]{:S(2)}, u32[]{:S(2)}) collective-permute-start(f32[3,256,256]{2,1,0:T(8,128)S(1)} %get-tuple-element.146), channel_id=1, source_target_pairs={{0,1},{1,2},{2,3},{4,5},{5,6},{6,7},{8,9},{9,10},{10,11},{12,13},{... | collective-permute-start | bytes 2359304 | tf_op jit(solution)/shard_map/ppermute | solution.py:19
  43.2 34.1 %collective-permute-start.5 = (f32[3,256,256]{2,1,0:T(8,128)S(1)}, f32[3,256,256]{2,1,0:T(8,128)}, u32[]{:S(2)}, u32[]{:S(2)}) collective-permute-start(f32[3,256,256]{2,1,0:T(8,128)S(1)} %get-tuple-element.147), channel_id=1, source_target_pairs={{0,5},{1,6},{2,7},{3,8},{4,9},{5,10},{6,11},{7,12},{8,13},{9,14},{... | collective-permute-start | bytes 2359304 | tf_op jit(solution)/shard_map/ppermute | solution.py:19
  56.1 37.4 %collective-permute-start.4 = (f32[3,256,256]{2,1,0:T(8,128)S(1)}, f32[3,256,256]{2,1,0:T(8,128)}, u32[]{:S(2)}, u32[]{:S(2)}) collective-permute-start(f32[3,256,256]{2,1,0:T(8,128)S(1)} %get-tuple-element.148), channel_id=1, source_target_pairs={{0,4},{4,8},{8,12},{12,16},{16,20},{20,24},{24,28},{1,5},{5,9},{9,... | collective-permute-start | bytes 2359304 | tf_op jit(solution)/shard_map/ppermute | solution.py:19
  59.6 300.3 %all-reduce.5.cloned.1.call-start = ((), (), s32[]{:S(2)}) async-start(), calls=%async_computation.1 | async-start | bytes 4194304 | tf_op jit(solution)/shard_map/psum | solution.py:258
  59.7 35.4 %copy-start.2 = (f32[2,256,256]{2,1,0:T(8,128)S(1)}, f32[2,256,256]{2,1,0:T(8,128)}, u32[]{:S(2)}) copy-start(f32[2,256,256]{2,1,0:T(8,128)} %home.1) | copy-start | bytes 1572868
  95.2 107.1 %copy-start = (f32[2,256,256]{2,1,0:T(8,128)}, f32[2,256,256]{2,1,0:T(8,128)S(1)}, u32[]{:S(2)}) copy-start(f32[2,256,256]{2,1,0:T(8,128)S(1)} %fusion.3.home) | copy-start | bytes 1572868
  95.2 107.1 %collective-permute-start.8 = (f32[2,256,256]{2,1,0:T(8,128)S(1)}, f32[2,256,256]{2,1,0:T(8,128)S(1)}, u32[]{:S(2)}, u32[]{:S(2)}) collective-permute-start(f32[2,256,256]{2,1,0:T(8,128)S(1)} %fusion.3.home), channel_id=1, source_target_pairs={{5,0},{6,1},{7,2},{8,3},{9,4},{10,5},{11,6},{12,7},{13,8},{14,9},{... | collective-permute-start | bytes 1572872 | tf_op jit(solution)/shard_map/ppermute | solution.py:19
  96.5 105.8 %collective-permute-start.7 = (f32[2,256,256]{2,1,0:T(8,128)S(1)}, f32[2,256,256]{2,1,0:T(8,128)S(1)}, u32[]{:S(2)}, u32[]{:S(2)}) collective-permute-start(f32[2,256,256]{2,1,0:T(8,128)S(1)} %fusion.3.home), channel_id=1, source_target_pairs={{4,0},{8,4},{12,8},{16,12},{20,16},{24,20},{28,24},{5,1},{9,5},{13... | collective-permute-start | bytes 1572872 | tf_op jit(solution)/shard_map/ppermute | solution.py:19
  97.8 104.5 %collective-permute-start.6 = (f32[2,256,256]{2,1,0:T(8,128)S(1)}, f32[2,256,256]{2,1,0:T(8,128)S(1)}, u32[]{:S(2)}, u32[]{:S(2)}) collective-permute-start(f32[2,256,256]{2,1,0:T(8,128)S(1)} %fusion.3.home), channel_id=1, source_target_pairs={{1,0},{2,1},{3,2},{5,4},{6,5},{7,6},{9,8},{10,9},{11,10},{13,12},{... | collective-permute-start | bytes 1572872 | tf_op jit(solution)/shard_map/ppermute | solution.py:19
  202.3 0.8 copy-start.6
  202.3 1.0 copy-start.7
  202.4 1.1 copy-start.8
  214.1 11.4 %collective-permute-start.9 = (f32[3,256,256]{2,1,0:T(8,128)S(1)}, f32[3,256,256]{2,1,0:T(8,128)S(1)}, u32[]{:S(2)}, u32[]{:S(2)}) collective-permute-start(f32[3,256,256]{2,1,0:T(8,128)S(1)} %get-tuple-element.143), channel_id=1, source_target_pairs={{0,1},{1,2},{2,3},{4,5},{5,6},{6,7},{8,9},{9,10},{10,11},{12,13},{... | collective-permute-start | bytes 2359304 | tf_op jit(solution)/shard_map/ppermute | solution.py:19
  215.5 26.9 %collective-permute-start.11 = (f32[3,256,256]{2,1,0:T(8,128)S(1)}, f32[3,256,256]{2,1,0:T(8,128)}, u32[]{:S(2)}, u32[]{:S(2)}) collective-permute-start(f32[3,256,256]{2,1,0:T(8,128)S(1)} %get-tuple-element.144), channel_id=1, source_target_pairs={{0,5},{1,6},{2,7},{3,8},{4,9},{5,10},{6,11},{7,12},{8,13},{9,14},{... | collective-permute-start | bytes 2359304 | tf_op jit(solution)/shard_map/ppermute | solution.py:19
  221.3 37.2 %collective-permute-start.10 = (f32[3,256,256]{2,1,0:T(8,128)S(1)}, f32[3,256,256]{2,1,0:T(8,128)}, u32[]{:S(2)}, u32[]{:S(2)}) collective-permute-start(f32[3,256,256]{2,1,0:T(8,128)S(1)} %get-tuple-element.145), channel_id=1, source_target_pairs={{0,4},{4,8},{8,12},{12,16},{16,20},{20,24},{24,28},{1,5},{5,9},{9,... | collective-permute-start | bytes 2359304 | tf_op jit(solution)/shard_map/ppermute | solution.py:19
  225.6 34.5 %copy-start.1 = (f32[2,256,256]{2,1,0:T(8,128)S(1)}, f32[2,256,256]{2,1,0:T(8,128)}, u32[]{:S(2)}) copy-start(f32[2,256,256]{2,1,0:T(8,128)} %copy-done) | copy-start | bytes 1572868
Sparse Core Ops, SparseCore 0:
  59.7 135.6 all-reduce.2
  225.7 134.2 all-reduce.4

commit v2 on v1

--- a/solution.py
+++ b/solution.py
@@ -1,3 +1,4 @@
+import functools
 import math
 
 import jax
@@ -11,12 +12,6 @@
 
 VMEM = pl.BlockSpec(memory_space=pltpu.VMEM)
 SMEM = pl.BlockSpec(memory_space=pltpu.SMEM)
-
-
-def from_behind(shard, axis, by):
-    size = lax.axis_size(axis)
-    pairs = [(i, i + by) for i in range(size) if 0 <= i + by < size]
-    return lax.ppermute(shard, axis, pairs)
 
 
 def make_tables(length):
@@ -43,20 +38,16 @@
 
 
 def frames_kernel(
-    count, offsets, weights, home, beyond, lower, corner, amplitudes, modes, rows_table, cols_table,
-    totals, mode_terms, stashed, wide,
+    count, offsets, weights, wide, amplitudes, modes, rows_table, cols_table,
+    totals, mode_terms, stashed,
 ):
     length = amplitudes.shape[1]
-    block_height, block_width = home.shape[1:]
     mode_count = modes.shape[0] // 2
-    wide[:, :block_height, :block_width] = home[...]
-    wide[:, :block_height, block_width:] = beyond[...]
-    wide[:, block_height:, :block_width] = lower[...]
-    wide[:, block_height:, block_width:] = corner[...]
+    full_width = wide.shape[2]
+    block_width = full_width - length
     totals[...] = jnp.zeros_like(totals)
     mode_terms[...] = jnp.zeros_like(mode_terms)
     stashed[...] = jnp.zeros_like(stashed)
-    full_width = block_width + length
 
     def visit(slot, carry):
         row, col = offsets[slot, 0], offsets[slot, 1]
@@ -206,16 +197,243 @@
             new_weights[g:g + 1, k:k + 1] = jnp.where(g < count[0], refit, kept)
 
 
-def settle(totals, block_height, block_width, length, col_index, col_count):
-    arrived = from_behind(totals[:, :block_height, block_width:], "col", 1)
-    lowered = from_behind(totals[:, block_height:, :block_width], "scan", 1)
-    corner = from_behind(totals[:, block_height:, block_width:], ("scan", "col"), col_count + 1)
-    corner = jnp.where(col_index > 0, corner, jnp.zeros_like(corner))
-    settled = totals[:, :block_height, :block_width]
-    settled = settled.at[:, :, :length].add(arrived)
-    settled = settled.at[:, :length, :].add(lowered)
-    settled = settled.at[:, :length, :length].add(corner)
-    return settled
+def reach(device, source, target, send_sem, recv_sem):
+    return pltpu.make_async_remote_copy(
+        src_ref=source,
+        dst_ref=target,
+        send_sem=send_sem,
+        recv_sem=recv_sem,
+        device_id=device,
+        device_id_type=pl.DeviceIdType.MESH,
+    )
+
+
+class Sides:
+    def __init__(self, scan_count, col_count):
+        self.scan, self.col = lax.axis_index("scan"), lax.axis_index("col")
+        self.right = (self.scan, lax.rem(self.col + 1, col_count))
+        self.left = (self.scan, lax.rem(self.col + col_count - 1, col_count))
+        self.down = (lax.rem(self.scan + 1, scan_count), self.col)
+        self.up = (lax.rem(self.scan + scan_count - 1, scan_count), self.col)
+        self.has_right, self.has_left = self.col < col_count - 1, self.col > 0
+        self.has_down, self.has_up = self.scan < scan_count - 1, self.scan > 0
+
+    def all(self):
+        return (
+            (self.right, self.has_right), (self.left, self.has_left),
+            (self.down, self.has_down), (self.up, self.has_up),
+        )
+
+
+def greet(sides, partners):
+    barrier = pltpu.get_barrier_semaphore()
+    for device in partners:
+        pl.semaphore_signal(barrier, inc=1, device_id=device, device_id_type=pl.DeviceIdType.MESH)
+    for device, there in sides.all():
+
+        @pl.when(there)
+        def _():
+            pl.semaphore_signal(
+                barrier, inc=1, device_id=device, device_id_type=pl.DeviceIdType.MESH
+            )
+
+    present = [there.astype(jnp.int32) for _, there in sides.all()]
+    pl.semaphore_wait(barrier, len(partners) + sum(present))
+
+
+class Shift:
+    def __init__(self, copy, sends, receives):
+        self.copy, self.sends, self.receives = copy, sends, receives
+
+    def start(self):
+        pl.when(self.sends)(self.copy.start)
+
+    def arrive(self):
+        pl.when(self.receives)(self.copy.wait_recv)
+
+    def leave(self):
+        pl.when(self.sends)(self.copy.wait_send)
+
+
+def halo_shifts(sides, wide, height, width, send_sems, recv_sems):
+    leftward = Shift(
+        reach(
+            sides.left, wide.at[:, pl.ds(0, height), pl.ds(0, width)],
+            wide.at[:, pl.ds(0, height), pl.ds(width, width)], send_sems.at[0], recv_sems.at[0],
+        ),
+        sides.has_left, sides.has_right,
+    )
+    upward = Shift(
+        reach(
+            sides.up, wide.at[:, pl.ds(0, height), :], wide.at[:, pl.ds(height, height), :],
+            send_sems.at[1], recv_sems.at[1],
+        ),
+        sides.has_up, sides.has_down,
+    )
+    return leftward, upward
+
+
+def blank_edges(sides, wide, height, width):
+    @pl.when(jnp.logical_not(sides.has_right))
+    def _():
+        wide[:, :height, width:] = jnp.zeros((wide.shape[0], height, width), jnp.float32)
+
+    @pl.when(jnp.logical_not(sides.has_down))
+    def _():
+        wide[:, height:, :] = jnp.zeros((wide.shape[0], height, 2 * width), jnp.float32)
+
+
+def halo_kernel(scan_count, col_count, field, wide, send_sems, recv_sems):
+    height, width = field.shape[1:]
+    sides = Sides(scan_count, col_count)
+    blank_edges(sides, wide, height, width)
+    wide[:, :height, :width] = field[...]
+    greet(sides, [])
+    leftward, upward = halo_shifts(sides, wide, height, width, send_sems, recv_sems)
+    leftward.start()
+    leftward.arrive()
+    upward.start()
+    upward.arrive()
+    leftward.leave()
+    upward.leave()
+
+
+def orders(scan_count, col_count):
+    scan_bits = [("scan", 1 << b) for b in range(scan_count.bit_length() - 1)]
+    col_bits = [("col", 1 << b) for b in range(col_count.bit_length() - 1)]
+    first, second = col_bits[:1], scan_bits[:1]
+    third, rest = col_bits[1:], scan_bits[1:]
+    return [first + second + third + rest, first + third + second + rest]
+
+
+def exchange_kernel(
+    scan_count, col_count, again, field, totals, terms, summed, result,
+    partial, landed, sideways, fallen, bottom, send_sems, recv_sems, side_send, side_recv,
+):
+    height, width = field.shape[1:]
+    sides = Sides(scan_count, col_count)
+    streams = orders(scan_count, col_count)
+    steps = len(streams[0])
+    share = terms.shape[0] // len(streams)
+
+    def partner(axis, bit):
+        at = sides.scan if axis == "scan" else sides.col
+        mine = at // bit % 2
+        other = at + bit - 2 * bit * mine
+        return mine, ((other, sides.col) if axis == "scan" else (sides.scan, other))
+
+    def blank(ref, absent):
+        @pl.when(absent)
+        def _():
+            ref[...] = jnp.zeros_like(ref)
+
+    blank(sideways, jnp.logical_not(sides.has_left))
+    blank(fallen, jnp.logical_not(sides.has_up))
+    if again:
+        blank_edges(sides, result, height, width)
+    greet(sides, [partner(axis, bit)[1] for axis, bit in streams[0]])
+
+    rightward = [
+        Shift(
+            reach(
+                sides.right, totals.at[:, pl.ds(at, height), pl.ds(width, width)],
+                sideways.at[:, pl.ds(at, height), :], side_send.at[k], side_recv.at[k],
+            ),
+            sides.has_right, sides.has_left,
+        )
+        for k, at in enumerate((height, 0))
+    ]
+    downward = Shift(
+        reach(sides.down, bottom, fallen, side_send.at[2], side_recv.at[2]), sides.has_down, sides.has_up
+    )
+    if again:
+        leftward, upward = halo_shifts(
+            sides, result, height, width, side_send.at[pl.ds(3, 2)], side_recv.at[pl.ds(3, 2)]
+        )
+
+    bases = [[t * share] for t in range(len(streams))]
+    halves = [share >> (s + 1) for s in range(steps)]
+    copies = {}
+
+    def rows(base, count):
+        return pl.ds(pl.multiple_of(base, 8), count)
+
+    def scatter_start(t, s):
+        mine, device = partner(*streams[t][s])
+        half = halves[s]
+        base = bases[t][s]
+        bases[t].append(base + mine * half)
+        source = terms if s == 0 else partial
+        copy = reach(
+            device, source.at[rows(base + (1 - mine) * half, half), :],
+            landed.at[pl.ds(t * share + share - 2 * half, half), :],
+            send_sems.at[t, s], recv_sems.at[t, s],
+        )
+        copy.start()
+        copies[t, s] = copy
+
+    def scatter_finish(t, s):
+        half = halves[s]
+        copies[t, s].wait_recv()
+        at = rows(bases[t][s + 1], half)
+        source = terms if s == 0 else partial
+        target = summed if s == steps - 1 else partial
+        target[at, :] = source[at, :] + landed[pl.ds(t * share + share - 2 * half, half), :]
+
+    def gather_start(t, s):
+        _, device = partner(*streams[t][s])
+        piece = summed.at[rows(bases[t][s + 1], halves[s]), :]
+        copy = reach(device, piece, piece, send_sems.at[t, steps + s], recv_sems.at[t, steps + s])
+        copy.start()
+        copies[t, steps + s] = copy
+
+    def drop():
+        rightward[0].arrive()
+        bottom[...] = totals[:, height:, :width] + sideways[:, height:, :]
+        downward.start()
+
+    def renew():
+        rightward[1].arrive()
+        downward.arrive()
+        sums = totals[:, :height, :width] + sideways[:, :height, :] + fallen[...]
+        fresh = field[...] + sums[:2] / (sums[2] + 1.0)
+        result[:, :height, :width] = fresh
+        if again:
+            leftward.start()
+
+    def lift():
+        if again:
+            leftward.arrive()
+            upward.start()
+
+    hooks = {1: drop, steps + steps // 2 - 1: renew, 2 * steps - 2: lift}
+    every = range(len(streams))
+    rightward[0].start()
+    for t in every:
+        scatter_start(t, 0)
+    rightward[1].start()
+    for s in range(steps):
+        for t in every:
+            scatter_finish(t, s)
+            if s < steps - 1:
+                scatter_start(t, s + 1)
+            else:
+                gather_start(t, s)
+        if s in hooks:
+            hooks[s]()
+    for s in range(steps - 1, -1, -1):
+        for t in every:
+            copies[t, steps + s].wait_recv()
+            if s > 0:
+                gather_start(t, s - 1)
+        if 2 * steps - 1 - s in hooks:
+            hooks[2 * steps - 1 - s]()
+    if again:
+        upward.arrive()
+    for copy in copies.values():
+        copy.wait_send()
+    for shift in rightward + [downward] + ([leftward, upward] if again else []):
+        shift.leave()
 
 
 def shape(*dims):
@@ -229,35 +447,69 @@
     block_height, block_width = object_field.shape[1:]
     scan_count = lax.axis_size("scan")
     col_count = lax.axis_size("col")
-    col_index = lax.axis_index("col")
-    block_corner = jnp.stack([lax.axis_index("scan") * block_height, col_index * block_width])
+    block_corner = jnp.stack(
+        [lax.axis_index("scan") * block_height, lax.axis_index("col") * block_width]
+    )
     offsets = positions - block_corner[None, :]
     root_total = math.sqrt(frames * scan_count * col_count)
     rows_table, cols_table = make_tables(length)
     modes = probe_modes.reshape(planes, length, length)
+    full_height, full_width = block_height + length, block_width + length
+    wide = pl.pallas_call(
+        functools.partial(halo_kernel, scan_count, col_count),
+        name="halo",
+        out_shape=shape(2, full_height, full_width),
+        in_specs=[VMEM],
+        out_specs=VMEM,
+        scratch_shapes=[pltpu.SemaphoreType.DMA((2,))] * 2,
+        compiler_params=pltpu.CompilerParams(collective_id=ITERS, has_side_effects=True),
+    )(object_field)
     for iteration in range(ITERS):
-        lower_rim = from_behind(object_field, "scan", -1)
-        beyond = from_behind(object_field, "col", -1)
-        corner = from_behind(object_field, ("scan", "col"), -(col_count + 1))
+        again = iteration < ITERS - 1
         totals, mode_terms, stashed = pl.pallas_call(
             frames_kernel,
             name="frames",
             out_shape=(
-                shape(3, block_height + length, block_width + length),
+                shape(3, full_height, full_width),
                 shape(planes, length, length),
                 shape(frames, 2, length, length),
             ),
-            in_specs=[SMEM] * 3 + [VMEM] * 8,
+            in_specs=[SMEM] * 3 + [VMEM] * 5,
             out_specs=(VMEM,) * 3,
-            scratch_shapes=[pltpu.VMEM((2, block_height + length, block_width + length), jnp.float32)],
             cost_estimate=pl.CostEstimate(flops=2 * 10**9, bytes_accessed=10**7, transcendentals=0),
         )(
-            frame_count, offsets, coefficients, object_field, beyond, lower_rim, corner, amplitudes,
-            modes, rows_table, cols_table,
+            frame_count, offsets, coefficients, wide, amplitudes, modes, rows_table, cols_table,
         )
-        summed = lax.psum(mode_terms, ("scan", "col"))
-        settled = settle(totals, block_height, block_width, length, col_index, col_count)
-        object_field = object_field + settled[:2] / (settled[2] + 1.0)
+        steps = scan_count.bit_length() + col_count.bit_length() - 2
+        rows = planes * length
+        summed, result = pl.pallas_call(
+            functools.partial(exchange_kernel, scan_count, col_count, again),
+            name="exchange",
+            out_shape=(
+                shape(rows, length),
+                shape(2, full_height, full_width) if again else shape(2, block_height, block_width),
+            ),
+            in_specs=[VMEM] * 3,
+            out_specs=(VMEM,) * 2,
+            scratch_shapes=[
+                pltpu.VMEM((rows, length), jnp.float32),
+                pltpu.VMEM((rows, length), jnp.float32),
+                pltpu.VMEM((3, full_height, length), jnp.float32),
+                pltpu.VMEM((3, length, block_width), jnp.float32),
+                pltpu.VMEM((3, length, block_width), jnp.float32),
+                pltpu.SemaphoreType.DMA((2, 2 * steps)),
+                pltpu.SemaphoreType.DMA((2, 2 * steps)),
+                pltpu.SemaphoreType.DMA((5,)),
+                pltpu.SemaphoreType.DMA((5,)),
+            ],
+            compiler_params=pltpu.CompilerParams(collective_id=iteration, has_side_effects=True),
+        )(object_field, totals, mode_terms.reshape(rows, length))
+        if again:
+            wide = result
+            object_field = result[:, :block_height, :block_width]
+        else:
+            object_field = result
+        summed = summed.reshape(planes, length, length)
         modes, coefficients = pl.pallas_call(
             lambda *refs: refit_kernel(root_total, *refs),
             name="refit",

time: 374 us -> 225 us (0.60)
  waiting for transfers between devices: 272 us -> 0 us
  Pallas kernels: 31.2 us -> 218 us
  starting transfers between devices: 40.9 us -> 0 us
  between operations: 14.9 us -> 1.33 us
  other arithmetic: 8.86 us -> 4.49 us
    psum x2 -> x0, waiting for transfers between devices: 195 us -> none  [on_device(): summed = lax.psum(mode_terms, ('scan', 'col'))]
    pallas_call x2 -> x5, Pallas kernels: 17.5 us -> 204 us  [the longest x2 161 us: on_device(): pl.pallas_call(functools.partial(exchange_kernel, scan_count, col_count,...]
    ppermute x12 -> x0, waiting for transfers between devices: 76.6 us -> none  [from_behind(): return lax.ppermute(shard, axis, pairs)]
    ppermute x12 -> x0, starting transfers between devices: 40.8 us -> none  [from_behind(): return lax.ppermute(shard, axis, pairs)]
    add x4 -> x0, other arithmetic: 4.28 us -> none  [the longest x2 3.31 us: settle(): settled = settled.at[:, :length, :length].add(corner)]
  transfers between devices with their start and end apart: 14 -> 0, of which waited for: 8 -> 0; matrix products, arithmetic and copies ran while one was open for 2% -> 0% of each run, Pallas kernels for 2% -> 0%
where the time goes in v2:
time: 225 us; the launch traced here: 226 us
  Pallas kernels  218 us (97%)
  other arithmetic  4.49 us (2%)
  local copies, waits for them, and re-layouts  2.67 us (1%)
    pallas_call x2, Pallas kernels, on_device(): pl.pallas_call(functools.partial(exchange_kernel, scan_count, col_count,...  161 us
    pallas_call x1, Pallas kernels, on_device(): pl.pallas_call(functools.partial(halo_kernel, scan_count, col_count), nam...  25.9 us
    pallas_call x2, Pallas kernels, on_device(): pl.pallas_call(frames_kernel, name='frames', out_shape=(shape(3, full_hei...  16.9 us
    pallas_call x2, Pallas kernels, on_device(): pl.pallas_call(lambda *refs: refit_kernel(root_total, *refs), name='refit...  13.8 us

profile of v2, /device:TPU:0, one launch (start us, length us, event | category | flops | bytes accessed | tf_op | source)
XLA Modules:
  0.0 226.2 jit_solution(16670730348045427615)
XLA Ops:
  0.6 1.1 negate_convert_fusion
  1.7 1.0 fusion.8
  2.7 1.1 fusion.1
  3.8 0.1 pad_add_fusion
  3.9 1.2 broadcast_subtract_fusion.offsets
  5.8 25.9 %halo.1.wide = f32[2,512,512]{2,1,0:T(8,128)} custom-call(f32[2,256,256]{2,1,0:T(8,128)} %field.3), custom_call_target="tpu_custom_call" | custom-call | tf_op jit(solution)/shard_map/halo/pallas_call | solution.py:458
  31.6 8.4 %frames.2 = (f32[3,512,512]{2,1,0:T(8,128)}, f32[8,256,256]{2,1,0:T(8,128)}, f32[2,2,256,256]{3,2,1,0:T(8,128)}) custom-call(s32[1]{0:T(128)S(6)} %copy.10.count.refs_0_, s32[2,2]{1,0:T(2,128)} %broadcast_subtract_fusion.offsets, f32[2,4]{1,0:T(2,128)} %refs_1_.1, f32[2,512,512]{2,1,0:T(8,128)} %halo.1.wide, bf16[2,256,256]{2,1,0:T(8,128)(2,1)} %amplitudes.3, ...), custom_call_target="tpu_custom_call" | custom-call | flops 2000000000 | bytes 10000000 | tf_op jit(solution)/shard_map/frames/pallas_call | solution.py:469
  40.1 92.8 %exchange.2 = (f32[2048,256]{1,0:T(8,128)}, f32[2,512,512]{2,1,0:T(8,128)}) custom-call(f32[2,256,256]{2,1,0:T(8,128)} %field.3, f32[3,512,512]{2,1,0:T(8,128)} %get-tuple-element.17.totals, f32[2048,256]{1,0:T(8,128)} %bitcast.13), custom_call_target="tpu_custom_call" | custom-call | tf_op jit(solution)/shard_map/exchange/pallas_call | solution.py:485
  132.9 6.9 %refit.2 = (f32[8,256,256]{2,1,0:T(8,128)}, f32[2,4]{1,0:T(2,128)}) custom-call(s32[1]{0:T(128)S(6)} %copy.10.count.refs_0_, f32[2,4]{1,0:T(2,128)} %refs_1_.1, f32[8,256,256]{2,1,0:T(8,128)} %bitcast.11, f32[8,256,256]{2,1,0:T(8,128)} %bitcast.9, f32[2,2,256,256]{3,2,1,0:T(8,128)} %get-tuple-element.21.refs_4_), custom_call_target="tpu_custom_call" | custom-call | tf_op jit(solution)/shard_map/refit/pallas_call | solution.py:513
  139.8 8.5 %frames.3 = (f32[3,512,512]{2,1,0:T(8,128)}, f32[8,256,256]{2,1,0:T(8,128)}, f32[2,2,256,256]{3,2,1,0:T(8,128)}) custom-call(s32[1]{0:T(128)S(6)} %copy.10.count.refs_0_, s32[2,2]{1,0:T(2,128)} %broadcast_subtract_fusion.offsets, f32[2,4]{1,0:T(2,128)} %get-tuple-element.22.weights.refs_1_, f32[2,512,512]{2,1,0:T(8,128)} %get-tuple-element.19.wide, ...), custom_call_target="tpu_custom_call" | custom-call | flops 2000000000 | bytes 10000000 | tf_op jit(solution)/shard_map/frames/pallas_call | solution.py:469
  148.2 1.9 slice.3.field
  150.1 68.4 %exchange.3 = (f32[2048,256]{1,0:T(8,128)}, f32[2,256,256]{2,1,0:T(8,128)}) custom-call(f32[2,256,256]{2,1,0:T(8,128)} %slice.3.field, f32[3,512,512]{2,1,0:T(8,128)} %get-tuple-element.24.totals, f32[2048,256]{1,0:T(8,128)} %bitcast.12), custom_call_target="tpu_custom_call" | custom-call | tf_op jit(solution)/shard_map/exchange/pallas_call | solution.py:485
  218.5 0.0 copy-start
  218.5 6.9 %refit.3 = (f32[8,256,256]{2,1,0:T(8,128)}, f32[2,4]{1,0:T(2,128)}) custom-call(s32[1]{0:T(128)S(6)} %copy.10.count.refs_0_, f32[2,4]{1,0:T(2,128)} %get-tuple-element.22.weights.refs_1_, f32[8,256,256]{2,1,0:T(8,128)} %bitcast.10, f32[8,256,256]{2,1,0:T(8,128)} %get-tuple-element.23.modes.refs_3_, f32[2,2,256,256]{3,2,1,0:T(8,128)} %get-tuple-element.28.refs_4_), custom_call_target="tpu_custom_call" | custom-call | tf_op jit(solution)/shard_map/refit/pallas_call | solution.py:513
  225.4 0.0 copy-done
  225.4 0.8 copy.11
Async XLA Ops:
  218.5 6.9 %copy-start = (f32[2,256,256]{2,1,0:T(8,128)S(1)}, f32[2,256,256]{2,1,0:T(8,128)}, u32[]{:S(2)}) copy-start(f32[2,256,256]{2,1,0:T(8,128)} %get-tuple-element.38) | copy-start | bytes 1572868

commit v3 on v2

--- a/solution.py
+++ b/solution.py
@@ -255,32 +255,59 @@
         pl.when(self.sends)(self.copy.wait_send)
 
 
-def halo_shifts(sides, wide, height, width, send_sems, recv_sems):
-    leftward = Shift(
-        reach(
-            sides.left, wide.at[:, pl.ds(0, height), pl.ds(0, width)],
-            wide.at[:, pl.ds(0, height), pl.ds(width, width)], send_sems.at[0], recv_sems.at[0],
-        ),
-        sides.has_left, sides.has_right,
-    )
-    upward = Shift(
-        reach(
-            sides.up, wide.at[:, pl.ds(0, height), :], wide.at[:, pl.ds(height, height), :],
-            send_sems.at[1], recv_sems.at[1],
-        ),
-        sides.has_up, sides.has_down,
-    )
-    return leftward, upward
+class Halo:
+    def __init__(self, sides, wide, height, width, send_sems, recv_sems):
+        top, low = pl.ds(0, height), pl.ds(height, height)
+        near, far = pl.ds(0, width), pl.ds(width, width)
+        planes = range(wide.shape[0])
+
+        def shift(device, source, target, at, sends, receives):
+            copy = reach(device, source, target, send_sems.at[at], recv_sems.at[at])
+            return Shift(copy, sends, receives)
+
+        self.side = shift(
+            sides.left, wide.at[:, top, near], wide.at[:, top, far], 0, sides.has_left, sides.has_right
+        )
+        self.up = [
+            shift(
+                sides.up, wide.at[p, top, near], wide.at[p, low, near], 1 + 2 * p,
+                sides.has_up, sides.has_down,
+            )
+            for p in planes
+        ]
+        self.corner = [
+            shift(
+                sides.left, wide.at[p, low, near], wide.at[p, low, far], 2 + 2 * p,
+                sides.has_left, sides.has_right,
+            )
+            for p in planes
+        ]
+
+    def begin(self):
+        for up in self.up:
+            up.start()
+        self.side.start()
+
+    def turn(self, plane):
+        self.up[plane].arrive()
+        self.corner[plane].start()
+
+    def end(self):
+        self.side.arrive()
+        for corner in self.corner:
+            corner.arrive()
+        for shift in [self.side] + self.up + self.corner:
+            shift.leave()
 
 
 def blank_edges(sides, wide, height, width):
     @pl.when(jnp.logical_not(sides.has_right))
     def _():
-        wide[:, :height, width:] = jnp.zeros((wide.shape[0], height, width), jnp.float32)
+        wide[:, :, width:] = jnp.zeros((wide.shape[0], 2 * height, width), jnp.float32)
 
     @pl.when(jnp.logical_not(sides.has_down))
     def _():
-        wide[:, height:, :] = jnp.zeros((wide.shape[0], height, 2 * width), jnp.float32)
+        wide[:, height:, :width] = jnp.zeros((wide.shape[0], height, width), jnp.float32)
 
 
 def halo_kernel(scan_count, col_count, field, wide, send_sems, recv_sems):
@@ -289,31 +316,36 @@
     blank_edges(sides, wide, height, width)
     wide[:, :height, :width] = field[...]
     greet(sides, [])
-    leftward, upward = halo_shifts(sides, wide, height, width, send_sems, recv_sems)
-    leftward.start()
-    leftward.arrive()
-    upward.start()
-    upward.arrive()
-    leftward.leave()
-    upward.leave()
+    halo = Halo(sides, wide, height, width, send_sems, recv_sems)
+    halo.begin()
+    for plane in range(wide.shape[0]):
+        halo.turn(plane)
+    halo.end()
 
 
 def orders(scan_count, col_count):
     scan_bits = [("scan", 1 << b) for b in range(scan_count.bit_length() - 1)]
     col_bits = [("col", 1 << b) for b in range(col_count.bit_length() - 1)]
-    first, second = col_bits[:1], scan_bits[:1]
-    third, rest = col_bits[1:], scan_bits[1:]
-    return [first + second + third + rest, first + third + second + rest]
+    core, col = col_bits[:1], col_bits[1:]
+    near, middle, far = scan_bits[:1], scan_bits[1:2], scan_bits[2:]
+    return [
+        core + col + near + middle + far,
+        core + middle + col + near + far,
+        core + near + col + middle + far,
+        core + col + middle + near + far,
+    ]
 
 
 def exchange_kernel(
     scan_count, col_count, again, field, totals, terms, summed, result,
     partial, landed, sideways, fallen, bottom, send_sems, recv_sems, side_send, side_recv,
 ):
-    height, width = field.shape[1:]
+    height, width = bottom.shape[1:]
     sides = Sides(scan_count, col_count)
     streams = orders(scan_count, col_count)
     steps = len(streams[0])
+    if terms.shape[0] // len(streams) >> steps < 8:
+        streams = streams[1:3]
     share = terms.shape[0] // len(streams)
 
     def partner(axis, bit):
@@ -333,23 +365,24 @@
         blank_edges(sides, result, height, width)
     greet(sides, [partner(axis, bit)[1] for axis, bit in streams[0]])
 
-    rightward = [
+    def rightward(at, band, target):
+        copy = reach(sides.right, band, target, side_send.at[at], side_recv.at[at])
+        return Shift(copy, sides.has_right, sides.has_left)
+
+    sums = range(totals.shape[0])
+    top, low = pl.ds(0, height), pl.ds(height, height)
+    beside = pl.ds(width, width)
+    rights = [rightward(p, totals.at[p, low, beside], sideways.at[p, low, :]) for p in sums]
+    last_right = rightward(3, totals.at[:, top, beside], sideways.at[:, top, :])
+    downs = [
         Shift(
-            reach(
-                sides.right, totals.at[:, pl.ds(at, height), pl.ds(width, width)],
-                sideways.at[:, pl.ds(at, height), :], side_send.at[k], side_recv.at[k],
-            ),
-            sides.has_right, sides.has_left,
+            reach(sides.down, bottom.at[p], fallen.at[p], side_send.at[4 + p], side_recv.at[4 + p]),
+            sides.has_down, sides.has_up,
         )
-        for k, at in enumerate((height, 0))
+        for p in sums
     ]
-    downward = Shift(
-        reach(sides.down, bottom, fallen, side_send.at[2], side_recv.at[2]), sides.has_down, sides.has_up
-    )
     if again:
-        leftward, upward = halo_shifts(
-            sides, result, height, width, side_send.at[pl.ds(3, 2)], side_recv.at[pl.ds(3, 2)]
-        )
+        halo = Halo(sides, result, height, width, side_send.at[pl.ds(7, 5)], side_recv.at[pl.ds(7, 5)])
 
     bases = [[t * share] for t in range(len(streams))]
     halves = [share >> (s + 1) for s in range(steps)]
@@ -387,31 +420,42 @@
         copy.start()
         copies[t, steps + s] = copy
 
-    def drop():
-        rightward[0].arrive()
-        bottom[...] = totals[:, height:, :width] + sideways[:, height:, :]
-        downward.start()
+    def drop(p):
+        rights[p].arrive()
+        bottom[p] = totals[p, height:, :width] + sideways[p, height:, :]
+        downs[p].start()
 
     def renew():
-        rightward[1].arrive()
-        downward.arrive()
-        sums = totals[:, :height, :width] + sideways[:, :height, :] + fallen[...]
-        fresh = field[...] + sums[:2] / (sums[2] + 1.0)
-        result[:, :height, :width] = fresh
+        last_right.arrive()
+        for down in downs:
+            down.arrive()
+        update = totals[:, :height, :width] + sideways[:, :height, :] + fallen[...]
+        result[:, :height, :width] = field[:, :height, :width] + update[:2] / (update[2] + 1.0)
         if again:
-            leftward.start()
-
-    def lift():
+            halo.begin()
+
+    def turn(p):
         if again:
-            leftward.arrive()
-            upward.start()
-
-    hooks = {1: drop, steps + steps // 2 - 1: renew, 2 * steps - 2: lift}
+            halo.turn(p)
+
+    hooks = {
+        0: [lambda: drop(0)],
+        1: [lambda: drop(1), lambda: drop(2)],
+        steps: [renew],
+        2 * steps - 3: [lambda: turn(0)],
+        2 * steps - 2: [lambda: turn(1)],
+    }
+
+    def run_hooks(at):
+        for hook in hooks.get(at, ()):
+            hook()
+
     every = range(len(streams))
-    rightward[0].start()
+    for right in rights:
+        right.start()
     for t in every:
         scatter_start(t, 0)
-    rightward[1].start()
+    last_right.start()
     for s in range(steps):
         for t in every:
             scatter_finish(t, s)
@@ -419,21 +463,19 @@
                 scatter_start(t, s + 1)
             else:
                 gather_start(t, s)
-        if s in hooks:
-            hooks[s]()
+        run_hooks(s)
     for s in range(steps - 1, -1, -1):
         for t in every:
             copies[t, steps + s].wait_recv()
             if s > 0:
                 gather_start(t, s - 1)
-        if 2 * steps - 1 - s in hooks:
-            hooks[2 * steps - 1 - s]()
-    if again:
-        upward.arrive()
+        run_hooks(2 * steps - 1 - s)
     for copy in copies.values():
         copy.wait_send()
-    for shift in rightward + [downward] + ([leftward, upward] if again else []):
+    for shift in rights + [last_right] + downs:
         shift.leave()
+    if again:
+        halo.end()
 
 
 def shape(*dims):
@@ -461,7 +503,7 @@
         out_shape=shape(2, full_height, full_width),
         in_specs=[VMEM],
         out_specs=VMEM,
-        scratch_shapes=[pltpu.SemaphoreType.DMA((2,))] * 2,
+        scratch_shapes=[pltpu.SemaphoreType.DMA((5,))] * 2,
         compiler_params=pltpu.CompilerParams(collective_id=ITERS, has_side_effects=True),
     )(object_field)
     for iteration in range(ITERS):
@@ -497,18 +539,14 @@
                 pltpu.VMEM((3, full_height, length), jnp.float32),
                 pltpu.VMEM((3, length, block_width), jnp.float32),
                 pltpu.VMEM((3, length, block_width), jnp.float32),
-                pltpu.SemaphoreType.DMA((2, 2 * steps)),
-                pltpu.SemaphoreType.DMA((2, 2 * steps)),
-                pltpu.SemaphoreType.DMA((5,)),
-                pltpu.SemaphoreType.DMA((5,)),
+                pltpu.SemaphoreType.DMA((4, 2 * steps)),
+                pltpu.SemaphoreType.DMA((4, 2 * steps)),
+                pltpu.SemaphoreType.DMA((12,)),
+                pltpu.SemaphoreType.DMA((12,)),
             ],
             compiler_params=pltpu.CompilerParams(collective_id=iteration, has_side_effects=True),
-        )(object_field, totals, mode_terms.reshape(rows, length))
-        if again:
-            wide = result
-            object_field = result[:, :block_height, :block_width]
-        else:
-            object_field = result
+        )(wide, totals, mode_terms.reshape(rows, length))
+        wide = result
         summed = summed.reshape(planes, length, length)
         modes, coefficients = pl.pallas_call(
             lambda *refs: refit_kernel(root_total, *refs),
@@ -518,7 +556,7 @@
             out_specs=(VMEM,) * 2,
             scratch_shapes=[pltpu.VMEM((planes, length, length), jnp.float32)],
         )(frame_count, coefficients, summed, modes, stashed)
-    return (object_field, modes.reshape(probe_modes.shape), coefficients)
+    return (wide, modes.reshape(probe_modes.shape), coefficients)
 
 
 def solution(mesh):

time: 225 us -> 209 us (0.929)
  Pallas kernels: 218 us -> 202 us
    pallas_call x2, Pallas kernels: 161 us -> 152 us  [on_device(): pl.pallas_call(functools.partial(exchange_kernel, scan_count, col_count,...]
    pallas_call x1, Pallas kernels: 25.9 us -> 19.7 us  [on_device(): pl.pallas_call(functools.partial(halo_kernel, scan_count, col_count), nam...]
where the time goes in v3:
time: 209 us
  Pallas kernels  202 us (97%)
  other arithmetic  4.49 us (2%)
    pallas_call x2, Pallas kernels, on_device(): pl.pallas_call(functools.partial(exchange_kernel, scan_count, col_count,...  152 us
    pallas_call x1, Pallas kernels, on_device(): pl.pallas_call(functools.partial(halo_kernel, scan_count, col_count), nam...  19.7 us
    pallas_call x2, Pallas kernels, on_device(): pl.pallas_call(frames_kernel, name='frames', out_shape=(shape(3, full_hei...  16.9 us
    pallas_call x2, Pallas kernels, on_device(): pl.pallas_call(lambda *refs: refit_kernel(root_total, *refs), name='refit...  13.8 us

profile of v3, /device:TPU:0, one launch (start us, length us, event | category | flops | bytes accessed | tf_op | source)
XLA Modules:
  0.0 208.9 jit_solution(6668635805565849617)
XLA Ops:
  1.3 0.1 pad_add_fusion
  1.4 1.2 broadcast_subtract_fusion.offsets
  2.6 1.0 fusion.8
  3.6 1.1 negate_convert_fusion
  4.7 1.1 fusion.1
  5.8 19.7 %halo.1.wide.field = f32[2,512,512]{2,1,0:T(8,128)} custom-call(f32[2,256,256]{2,1,0:T(8,128)} %field.1), custom_call_target="tpu_custom_call" | custom-call | tf_op jit(solution)/shard_map/halo/pallas_call | solution.py:500
  25.5 8.4 %frames.2 = (f32[3,512,512]{2,1,0:T(8,128)}, f32[8,256,256]{2,1,0:T(8,128)}, f32[2,2,256,256]{3,2,1,0:T(8,128)}) custom-call(s32[1]{0:T(128)S(6)} %copy.10.count.refs_0_, s32[2,2]{1,0:T(2,128)} %broadcast_subtract_fusion.offsets, f32[2,4]{1,0:T(2,128)} %refs_1_.1, f32[2,512,512]{2,1,0:T(8,128)} %halo.1.wide.field, bf16[2,256,256]{2,1,0:T(8,128)(2,1)} %amplitudes.3, ...), custom_call_target="tpu_custom_call" | custom-call | flops 2000000000 | bytes 10000000 | tf_op jit(solution)/shard_map/frames/pallas_call | solution.py:511
  34.0 88.0 %exchange.2 = (f32[2048,256]{1,0:T(8,128)}, f32[2,512,512]{2,1,0:T(8,128)}) custom-call(f32[2,512,512]{2,1,0:T(8,128)} %halo.1.wide.field, f32[3,512,512]{2,1,0:T(8,128)} %get-tuple-element.17.totals, f32[2048,256]{1,0:T(8,128)} %bitcast.9), custom_call_target="tpu_custom_call" | custom-call | tf_op jit(solution)/shard_map/exchange/pallas_call | solution.py:527
  122.0 6.9 %refit.2 = (f32[8,256,256]{2,1,0:T(8,128)}, f32[2,4]{1,0:T(2,128)}) custom-call(s32[1]{0:T(128)S(6)} %copy.10.count.refs_0_, f32[2,4]{1,0:T(2,128)} %refs_1_.1, f32[8,256,256]{2,1,0:T(8,128)} %bitcast.13, f32[8,256,256]{2,1,0:T(8,128)} %bitcast.11, f32[2,2,256,256]{3,2,1,0:T(8,128)} %get-tuple-element.21.refs_4_), custom_call_target="tpu_custom_call" | custom-call | tf_op jit(solution)/shard_map/refit/pallas_call | solution.py:551
  128.9 8.4 %frames.3 = (f32[3,512,512]{2,1,0:T(8,128)}, f32[8,256,256]{2,1,0:T(8,128)}, f32[2,2,256,256]{3,2,1,0:T(8,128)}) custom-call(s32[1]{0:T(128)S(6)} %copy.10.count.refs_0_, s32[2,2]{1,0:T(2,128)} %broadcast_subtract_fusion.offsets, f32[2,4]{1,0:T(2,128)} %get-tuple-element.22.weights.refs_1_, f32[2,512,512]{2,1,0:T(8,128)} %get-tuple-element.19.wide.field, ...), custom_call_target="tpu_custom_call" | custom-call | flops 2000000000 | bytes 10000000 | tf_op jit(solution)/shard_map/frames/pallas_call | solution.py:511
  137.3 63.8 %exchange.3 = (f32[2048,256]{1,0:T(8,128)}, f32[2,256,256]{2,1,0:T(8,128)}) custom-call(f32[2,512,512]{2,1,0:T(8,128)} %get-tuple-element.19.wide.field, f32[3,512,512]{2,1,0:T(8,128)} %get-tuple-element.24.totals, f32[2048,256]{1,0:T(8,128)} %bitcast.8), custom_call_target="tpu_custom_call" | custom-call | tf_op jit(solution)/shard_map/exchange/pallas_call | solution.py:527
  201.2 0.0 copy-start
  201.2 6.9 %refit.3 = (f32[8,256,256]{2,1,0:T(8,128)}, f32[2,4]{1,0:T(2,128)}) custom-call(s32[1]{0:T(128)S(6)} %copy.10.count.refs_0_, f32[2,4]{1,0:T(2,128)} %get-tuple-element.22.weights.refs_1_, f32[8,256,256]{2,1,0:T(8,128)} %bitcast.12, f32[8,256,256]{2,1,0:T(8,128)} %get-tuple-element.23.modes.refs_3_, f32[2,2,256,256]{3,2,1,0:T(8,128)} %get-tuple-element.28.refs_4_), custom_call_target="tpu_custom_call" | custom-call | tf_op jit(solution)/shard_map/refit/pallas_call | solution.py:551
  208.1 0.0 copy-done
  208.1 0.8 copy.11
Async XLA Ops:
  201.2 6.9 %copy-start = (f32[2,256,256]{2,1,0:T(8,128)S(1)}, f32[2,256,256]{2,1,0:T(8,128)}, u32[]{:S(2)}) copy-start(f32[2,256,256]{2,1,0:T(8,128)} %get-tuple-element.38) | copy-start | bytes 1572868

commit v4 on v3

--- a/solution.py
+++ b/solution.py
@@ -438,12 +438,15 @@
         if again:
             halo.turn(p)
 
+    def shove():
+        for right in rights:
+            right.start()
+
     hooks = {
-        0: [lambda: drop(0)],
-        1: [lambda: drop(1), lambda: drop(2)],
-        steps: [renew],
-        2 * steps - 3: [lambda: turn(0)],
-        2 * steps - 2: [lambda: turn(1)],
+        1: [shove],
+        steps - 2: [lambda: drop(0)],
+        steps - 1: [lambda: drop(1), lambda: drop(2), last_right.start],
+        2 * steps - 1: [renew, lambda: turn(0), lambda: turn(1)],
     }
 
     def run_hooks(at):
@@ -451,11 +454,8 @@
             hook()
 
     every = range(len(streams))
-    for right in rights:
-        right.start()
     for t in every:
         scatter_start(t, 0)
-    last_right.start()
     for s in range(steps):
         for t in every:
             scatter_finish(t, s)

time: 209 us -> 191 us (0.914)
  Pallas kernels: 202 us -> 183 us
    pallas_call x2, Pallas kernels: 152 us -> 132 us  [on_device(): pl.pallas_call(functools.partial(exchange_kernel, scan_count, col_count,...]
where the time goes in v4:
time: 191 us; the launch traced here: 189 us
  Pallas kernels  183 us (96%)
  other arithmetic  4.49 us (2%)
    pallas_call x2, Pallas kernels, on_device(): pl.pallas_call(functools.partial(exchange_kernel, scan_count, col_count,...  132 us
    pallas_call x1, Pallas kernels, on_device(): pl.pallas_call(functools.partial(halo_kernel, scan_count, col_count), nam...  19.7 us
    pallas_call x2, Pallas kernels, on_device(): pl.pallas_call(frames_kernel, name='frames', out_shape=(shape(3, full_hei...  16.9 us
    pallas_call x2, Pallas kernels, on_device(): pl.pallas_call(lambda *refs: refit_kernel(root_total, *refs), name='refit...  13.8 us

profile of v4, /device:TPU:0, one launch (start us, length us, event | category | flops | bytes accessed | tf_op | source)
XLA Modules:
  0.0 189.2 jit_solution(5500462486206968520)
XLA Ops:
  1.3 0.1 pad_add_fusion
  1.4 1.2 broadcast_subtract_fusion.offsets
  2.6 1.0 fusion.8
  3.6 1.1 negate_convert_fusion
  4.7 1.1 fusion.1
  5.8 19.7 %halo.1.wide.field = f32[2,512,512]{2,1,0:T(8,128)} custom-call(f32[2,256,256]{2,1,0:T(8,128)} %field.1), custom_call_target="tpu_custom_call" | custom-call | tf_op jit(solution)/shard_map/halo/pallas_call | solution.py:500
  25.5 8.4 %frames.2 = (f32[3,512,512]{2,1,0:T(8,128)}, f32[8,256,256]{2,1,0:T(8,128)}, f32[2,2,256,256]{3,2,1,0:T(8,128)}) custom-call(s32[1]{0:T(128)S(6)} %copy.10.count.refs_0_, s32[2,2]{1,0:T(2,128)} %broadcast_subtract_fusion.offsets, f32[2,4]{1,0:T(2,128)} %refs_1_.1, f32[2,512,512]{2,1,0:T(8,128)} %halo.1.wide.field, bf16[2,256,256]{2,1,0:T(8,128)(2,1)} %amplitudes.3, ...), custom_call_target="tpu_custom_call" | custom-call | flops 2000000000 | bytes 10000000 | tf_op jit(solution)/shard_map/frames/pallas_call | solution.py:511
  34.0 71.9 %exchange.2 = (f32[2048,256]{1,0:T(8,128)}, f32[2,512,512]{2,1,0:T(8,128)}) custom-call(f32[2,512,512]{2,1,0:T(8,128)} %halo.1.wide.field, f32[3,512,512]{2,1,0:T(8,128)} %get-tuple-element.17.totals, f32[2048,256]{1,0:T(8,128)} %bitcast.9), custom_call_target="tpu_custom_call" | custom-call | tf_op jit(solution)/shard_map/exchange/pallas_call | solution.py:527
  105.8 6.9 %refit.2 = (f32[8,256,256]{2,1,0:T(8,128)}, f32[2,4]{1,0:T(2,128)}) custom-call(s32[1]{0:T(128)S(6)} %copy.10.count.refs_0_, f32[2,4]{1,0:T(2,128)} %refs_1_.1, f32[8,256,256]{2,1,0:T(8,128)} %bitcast.13, f32[8,256,256]{2,1,0:T(8,128)} %bitcast.11, f32[2,2,256,256]{3,2,1,0:T(8,128)} %get-tuple-element.21.refs_4_), custom_call_target="tpu_custom_call" | custom-call | tf_op jit(solution)/shard_map/refit/pallas_call | solution.py:551
  112.7 8.4 %frames.3 = (f32[3,512,512]{2,1,0:T(8,128)}, f32[8,256,256]{2,1,0:T(8,128)}, f32[2,2,256,256]{3,2,1,0:T(8,128)}) custom-call(s32[1]{0:T(128)S(6)} %copy.10.count.refs_0_, s32[2,2]{1,0:T(2,128)} %broadcast_subtract_fusion.offsets, f32[2,4]{1,0:T(2,128)} %get-tuple-element.22.weights.refs_1_, f32[2,512,512]{2,1,0:T(8,128)} %get-tuple-element.19.wide.field, ...), custom_call_target="tpu_custom_call" | custom-call | flops 2000000000 | bytes 10000000 | tf_op jit(solution)/shard_map/frames/pallas_call | solution.py:511
  121.1 60.4 %exchange.3 = (f32[2048,256]{1,0:T(8,128)}, f32[2,256,256]{2,1,0:T(8,128)}) custom-call(f32[2,512,512]{2,1,0:T(8,128)} %get-tuple-element.19.wide.field, f32[3,512,512]{2,1,0:T(8,128)} %get-tuple-element.24.totals, f32[2048,256]{1,0:T(8,128)} %bitcast.8), custom_call_target="tpu_custom_call" | custom-call | tf_op jit(solution)/shard_map/exchange/pallas_call | solution.py:527
  181.5 0.0 copy-start
  181.5 6.9 %refit.3 = (f32[8,256,256]{2,1,0:T(8,128)}, f32[2,4]{1,0:T(2,128)}) custom-call(s32[1]{0:T(128)S(6)} %copy.10.count.refs_0_, f32[2,4]{1,0:T(2,128)} %get-tuple-element.22.weights.refs_1_, f32[8,256,256]{2,1,0:T(8,128)} %bitcast.12, f32[8,256,256]{2,1,0:T(8,128)} %get-tuple-element.23.modes.refs_3_, f32[2,2,256,256]{3,2,1,0:T(8,128)} %get-tuple-element.28.refs_4_), custom_call_target="tpu_custom_call" | custom-call | tf_op jit(solution)/shard_map/refit/pallas_call | solution.py:551
  188.4 0.0 copy-done
  188.4 0.8 copy.11
Async XLA Ops:
  181.5 6.9 %copy-start = (f32[2,256,256]{2,1,0:T(8,128)S(1)}, f32[2,256,256]{2,1,0:T(8,128)}, u32[]{:S(2)}) copy-start(f32[2,256,256]{2,1,0:T(8,128)} %get-tuple-element.38) | copy-start | bytes 1572868
